TPU v7x, 1024 devices: a whole 8x8x8 slice. The times are simulated.
1024 devices in a mesh: px: 8 (over y), py: 64 (over x_hi, z, core), lev: 2 (over x_lo).
Axes of the slice: x: 8 (x_hi: 4, x_lo: 2; x = x_hi * 2 + x_lo), y: 8, z: 8, core: 2. Of those that a mesh axis runs over, the one named last changes fastest.
Arguments:
- tracer: float32 [2, 8, 64, 8192], P('lev', None, 'px', 'py'), may hold values from -6 to 6
- node_mass: float32 [2, 64, 8192], P('lev', 'px', 'py'), may hold values from 0.5 to 2
- wind_x: float32 [2, 64, 8192], P('lev', 'px', 'py'), may hold values from -4 to 4
- wind_y: float32 [2, 64, 8192], P('lev', 'px', 'py'), may hold values from -4 to 4
- remap: float32 [2, 2], replicated, may hold values from -4 to 4
Outputs:
- remapped: float32 [2, 8, 64, 8192], P(None, 'lev', 'px', 'py')
All inputs are finite; a program needn't handle non-finite values.
Results may differ from a plain program's by a relative error of at most 0.0001.
Values sent between devices are 32-bit elements; how exact they have to be, the bound alone decides.
No kernel may reach another device: no remote copies, remote signals or barrier semaphores. Data moves between devices by JAX's collectives and lax.ppermute only.
A program may use at most 32 MiB of HBM per device.

v0:
```python
import jax
import jax.numpy as jnp
import numpy as np
from jax import lax
from jax.sharding import PartitionSpec as P

GLL_NODES = 4


sentinel = 1e30
step_size = 0.1
section_weights = ((0.0, 1.0), (0.75, 0.25), (1.0 / 3.0, 2.0 / 3.0))


def extended(block, sides, width):
    for axis, dim in sides:
        count = lax.axis_size(axis)
        forward = [(i, i + 1) for i in range(count - 1)]
        forward.append((count - 1, 0))
        backward = [(target, source) for source, target in forward]
        low = lax.ppermute(
            lax.slice_in_dim(block, block.shape[dim] - width, None, axis=dim), axis, forward
        )
        high = lax.ppermute(lax.slice_in_dim(block, 0, width, axis=dim), axis, backward)
        block = jnp.concatenate([low, block, high], axis=dim)
    return block


def derivative_table():
    points = np.array([-1.0, -(5.0 ** (-0.5)), 5.0 ** (-0.5), 1.0])
    number = points.shape[0]
    barycentric = np.array(
        [
            1.0
            / np.prod([points[outer] - points[inner] for inner in range(number) if inner != outer])
            for outer in range(number)
        ]
    )
    table = np.zeros((number, number))
    for outer in range(number):
        for inner in range(number):
            if inner != outer:
                table[outer, inner] = (
                    barycentric[inner] / barycentric[outer] / (points[outer] - points[inner])
                )
    for outer in range(number):
        table[outer, outer] = -np.sum(table[outer])
    return table


def block_table(elements):
    return jnp.asarray(np.kron(np.eye(elements), derivative_table()), jnp.float32)


def pair_sum(values, which_axis):
    layout = values.shape
    where_at = len(layout) + which_axis
    elements = layout[where_at] // GLL_NODES
    blocked = values.reshape(layout[:where_at] + (elements, GLL_NODES) + layout[where_at + 1 :])
    head_nodes = lax.slice_in_dim(blocked, 0, 1, axis=where_at + 1)
    tail_nodes = lax.slice_in_dim(blocked, GLL_NODES - 1, GLL_NODES, axis=where_at + 1)
    middle = lax.slice_in_dim(blocked, 1, GLL_NODES - 1, axis=where_at + 1)
    zero_slab = jnp.zeros_like(lax.slice_in_dim(tail_nodes, 0, 1, axis=where_at))
    before = jnp.concatenate(
        [zero_slab, lax.slice_in_dim(tail_nodes, 0, elements - 1, axis=where_at)], axis=where_at
    )
    following = jnp.concatenate(
        [lax.slice_in_dim(head_nodes, 1, elements, axis=where_at), zero_slab], axis=where_at
    )
    joined = jnp.concatenate(
        [head_nodes + before, middle, tail_nodes + following], axis=where_at + 1
    )
    return joined.reshape(layout)


def shared_ext(values, width, keep_rim):
    filler = (GLL_NODES - width % GLL_NODES) % GLL_NODES
    padded = jnp.pad(values, [(0, 0)] * (values.ndim - 2) + [(filler, filler), (filler, filler)])
    summed = pair_sum(pair_sum(padded, -2), -1)
    margin = filler + width - keep_rim
    return summed[..., margin : summed.shape[-2] - margin, margin : summed.shape[-1] - margin]


def edge_cut(values, width, fill_value):
    columns = lax.broadcasted_iota(jnp.int32, values.shape, values.ndim - 1)
    position = lax.axis_index("py")
    cut_mask = (columns < width) & (position == 0) | (columns >= values.shape[-1] - width) & (
        position == lax.axis_size("py") - 1
    )
    return jnp.where(cut_mask, fill_value, values)


def element_extrema(field):
    layout = field.shape
    blocked = field.reshape(
        layout[0], layout[1], layout[2] // GLL_NODES, GLL_NODES, layout[3] // GLL_NODES, GLL_NODES
    )
    return jnp.stack([jnp.min(blocked, axis=(3, 5)), -jnp.max(blocked, axis=(3, 5))])


def bounded(padded):
    rows_min = jnp.minimum(
        jnp.minimum(padded[..., :-2, :], padded[..., 1:-1, :]), padded[..., 2:, :]
    )
    result = jnp.minimum(jnp.minimum(rows_min[..., :-2], rows_min[..., 1:-1]), rows_min[..., 2:])
    return (result[0], -result[1])


def tendency(field, wind_x, wind_y, table_x, table_y):
    slope_x = jnp.einsum(
        "ij,lcjy->lciy", table_x, wind_x[:, None] * field, precision=lax.Precision.HIGHEST
    )
    slope_y = jnp.einsum(
        "lcxj,ij->lcxi", wind_y[:, None] * field, table_y, precision=lax.Precision.HIGHEST
    )
    return field - step_size * (slope_x + slope_y)


def limit(moved, lower, upper):
    layout = moved.shape
    blocked = moved.reshape(
        layout[0], layout[1], layout[2] // GLL_NODES, GLL_NODES, layout[3] // GLL_NODES, GLL_NODES
    )
    clipped = jnp.clip(blocked, lower[:, :, :, None, :, None], upper[:, :, :, None, :, None])
    return clipped.reshape(layout)


def shards(tracer, node_mass, wind_x, wind_y, remap):
    table_x = block_table(tracer.shape[2] // GLL_NODES)
    table_y = block_table(tracer.shape[3] // GLL_NODES)
    rim_width = GLL_NODES + 1
    keep_rim = GLL_NODES
    mass_ext = extended(node_mass, (("px", 1), ("py", 2)), rim_width)
    mass_sum = shared_ext(edge_cut(mass_ext, rim_width, 0.0), rim_width, keep_rim)
    mass_sum = edge_cut(mass_sum, keep_rim, 1.0)
    start = extended(tracer, (("px", 2), ("py", 3)), GLL_NODES)
    field = start
    for share_start, share_new in section_weights:
        lower, upper = bounded(edge_cut(element_extrema(field), 1, sentinel))
        inner = field[:, :, GLL_NODES:-GLL_NODES, GLL_NODES:-GLL_NODES]
        limited = limit(tendency(inner, wind_x, wind_y, table_x, table_y), lower, upper)
        weighted = node_mass[:, None] * limited
        weighted_ext = extended(weighted, (("px", 2), ("py", 3)), GLL_NODES + 1)
        summed = shared_ext(edge_cut(weighted_ext, GLL_NODES + 1, 0.0), GLL_NODES + 1, GLL_NODES)
        field = share_start * start + share_new * (summed / mass_sum[:, None])
    field = field[:, :, GLL_NODES:-GLL_NODES, GLL_NODES:-GLL_NODES]
    return jnp.einsum(
        "ab,bcxy->acxy",
        remap,
        lax.all_to_all(field, "lev", split_axis=1, concat_axis=0, tiled=True),
        precision=lax.Precision.HIGHEST,
    )


def solution(mesh):
    in_specs = (
        P("lev", None, "px", "py"),
        P("lev", "px", "py"),
        P("lev", "px", "py"),
        P("lev", "px", "py"),
        P(),
    )
    out_specs = P(None, "lev", "px", "py")
    return jax.shard_map(shards, mesh=mesh, in_specs=in_specs, out_specs=out_specs, check_vma=False)
```

profile of v0, /device:TPU:16, one launch (start us, length us, event | category | flops | bytes accessed | tf_op | source)
XLA Modules:
  0.0 151.5 jit_solution(10165834193945445712)
XLA Ops:
  0.8 3.6 %collective-permute-start.8 = (f32[1,5,128]{2,1,0:T(8,128)S(1)}, f32[1,5,128]{2,1,0:T(8,128)S(1)}, u32[]{:S(2)}, u32[]{:S(2)}) collective-permute-start(f32[1,5,128]{2,1,0:T(8,128)S(1)} %get-tuple-element.67), channel_id=1, source_target_pairs={{0,128},{128,256},{256,384},{384,512},{512,640},{640,768},{768,896... | collective-permute-start | bytes 7688 | tf_op jit(solution)/shard_map/ppermute | solution.py:21
  4.4 13.2 %collective-permute-start.9 = (f32[1,5,128]{2,1,0:T(8,128)S(1)}, f32[1,5,128]{2,1,0:T(8,128)S(1)}, u32[]{:S(2)}, u32[]{:S(2)}) collective-permute-start(f32[1,5,128]{2,1,0:T(8,128)S(1)} %get-tuple-element.68), channel_id=1, source_target_pairs={{128,0},{256,128},{384,256},{512,384},{640,512},{768,640},{896,768... | collective-permute-start | bytes 7688 | tf_op jit(solution)/shard_map/ppermute | solution.py:24
  20.3 5.1 %collective-permute-start.1 = (f32[1,8,4,128]{3,2,1,0:T(4,128)S(1)}, f32[1,8,4,128]{3,2,1,0:T(4,128)S(1)}, u32[]{:S(2)}, u32[]{:S(2)}) collective-permute-start(f32[1,8,4,128]{3,2,1,0:T(4,128)S(1)} %get-tuple-element.54), channel_id=1, source_target_pairs={{128,0},{256,128},{384,256},{512,384},{640,512},{768,640},{896,768... | collective-permute-start | bytes 49160 | tf_op jit(solution)/shard_map/ppermute | solution.py:24
  29.2 7.9 %collective-permute-start.11 = (f32[1,18,5]{2,1,0:T(8,128)S(1)}, f32[1,18,5]{2,1,0:T(8,128)S(1)}, u32[]{:S(2)}, u32[]{:S(2)}) collective-permute-start(f32[1,18,5]{2,1,0:T(8,128)S(1)} %get-tuple-element.66), channel_id=1, source_target_pairs={{2,0},{4,2},{6,4},{8,6},{10,8},{12,10},{14,12},{16,14},{18,16},{20... | collective-permute-start | bytes 1088 | tf_op jit(solution)/shard_map/ppermute | solution.py:24
  39.9 1.9 %collective-permute-start.2 = (f32[1,8,16,4]{3,2,1,0:T(8,128)S(1)}, f32[1,8,16,4]{3,2,1,0:T(8,128)S(1)}, u32[]{:S(2)}, u32[]{:S(2)}) collective-permute-start(f32[1,8,16,4]{3,2,1,0:T(8,128)S(1)} %get-tuple-element.45), channel_id=1, source_target_pairs={{0,2},{2,4},{4,6},{6,8},{8,10},{10,12},{12,14},{14,16},{16,18},{18... | collective-permute-start | bytes 6152 | tf_op jit(solution)/shard_map/ppermute | solution.py:21
  41.8 7.9 %collective-permute-start.3 = (f32[1,8,16,4]{3,2,1,0:T(8,128)S(1)}, f32[1,8,16,4]{3,2,1,0:T(8,128)S(1)}, u32[]{:S(2)}, u32[]{:S(2)}) collective-permute-start(f32[1,8,16,4]{3,2,1,0:T(8,128)S(1)} %get-tuple-element.46), channel_id=1, source_target_pairs={{2,0},{4,2},{6,4},{8,6},{10,8},{12,10},{14,12},{16,14},{18,16},{20... | collective-permute-start | bytes 6152 | tf_op jit(solution)/shard_map/ppermute | solution.py:24
  50.2 2.0 %collective-permute-done.3 = f32[1,8,16,4]{3,2,1,0:T(8,128)S(1)} collective-permute-done((f32[1,8,16,4]{3,2,1,0:T(8,128)S(1)}, f32[1,8,16,4]{3,2,1,0:T(8,128)S(1)}, u32[]{:S(2)}, u32[]{:S(2)}) %collective-permute-start.3) | collective-permute-done | bytes 2080 | tf_op jit(solution)/shard_map/ppermute | solution.py:24
  54.6 3.6 %collective-permute-start.4 = (f32[1,8,5,128]{3,2,1,0:T(8,128)S(1)}, f32[1,8,5,128]{3,2,1,0:T(8,128)S(1)}, u32[]{:S(2)}, u32[]{:S(2)}) collective-permute-start(f32[1,8,5,128]{3,2,1,0:T(8,128)S(1)} %get-tuple-element.51), channel_id=1, source_target_pairs={{0,128},{128,256},{256,384},{384,512},{512,640},{640,768},{768,896... | collective-permute-start | bytes 61448 | tf_op jit(solution)/shard_map/ppermute | solution.py:21
  58.2 3.2 %collective-permute-start.5 = (f32[1,8,5,128]{3,2,1,0:T(8,128)S(1)}, f32[1,8,5,128]{3,2,1,0:T(8,128)S(1)}, u32[]{:S(2)}, u32[]{:S(2)}) collective-permute-start(f32[1,8,5,128]{3,2,1,0:T(8,128)S(1)} %get-tuple-element.52), channel_id=1, source_target_pairs={{128,0},{256,128},{384,256},{512,384},{640,512},{768,640},{896,768... | collective-permute-start | bytes 61448 | tf_op jit(solution)/shard_map/ppermute | solution.py:24
  62.1 2.9 %collective-permute-done.5 = f32[1,8,5,128]{3,2,1,0:T(8,128)S(1)} collective-permute-done((f32[1,8,5,128]{3,2,1,0:T(8,128)S(1)}, f32[1,8,5,128]{3,2,1,0:T(8,128)S(1)}, u32[]{:S(2)}, u32[]{:S(2)}) %collective-permute-start.5) | collective-permute-done | bytes 20512 | tf_op jit(solution)/shard_map/ppermute | solution.py:24
  65.1 1.9 %collective-permute-start.6 = (f32[1,8,18,5]{3,2,1,0:T(8,128)S(1)}, f32[1,8,18,5]{3,2,1,0:T(8,128)S(1)}, u32[]{:S(2)}, u32[]{:S(2)}) collective-permute-start(f32[1,8,18,5]{3,2,1,0:T(8,128)S(1)} %get-tuple-element.43), channel_id=1, source_target_pairs={{0,2},{2,4},{4,6},{6,8},{8,10},{10,12},{12,14},{14,16},{16,18},{18... | collective-permute-start | bytes 8648 | tf_op jit(solution)/shard_map/ppermute | solution.py:21
  67.0 7.9 %collective-permute-start.7 = (f32[1,8,18,5]{3,2,1,0:T(8,128)S(1)}, f32[1,8,18,5]{3,2,1,0:T(8,128)S(1)}, u32[]{:S(2)}, u32[]{:S(2)}) collective-permute-start(f32[1,8,18,5]{3,2,1,0:T(8,128)S(1)} %get-tuple-element.44), channel_id=1, source_target_pairs={{2,0},{4,2},{6,4},{8,6},{10,8},{12,10},{14,12},{16,14},{18,16},{20... | collective-permute-start | bytes 8648 | tf_op jit(solution)/shard_map/ppermute | solution.py:24
  75.2 2.3 %collective-permute-done.7 = f32[1,8,18,5]{3,2,1,0:T(8,128)S(1)} collective-permute-done((f32[1,8,18,5]{3,2,1,0:T(8,128)S(1)}, f32[1,8,18,5]{3,2,1,0:T(8,128)S(1)}, u32[]{:S(2)}, u32[]{:S(2)}) %collective-permute-start.7) | collective-permute-done | bytes 2912 | tf_op jit(solution)/shard_map/ppermute | solution.py:24
  85.5 4.9 %collective-permute-start.12 = (f32[1,8,5,128]{3,2,1,0:T(8,128)S(1)}, f32[1,8,5,128]{3,2,1,0:T(8,128)S(1)}, u32[]{:S(2)}, u32[]{:S(2)}) collective-permute-start(f32[1,8,5,128]{3,2,1,0:T(8,128)S(1)} %get-tuple-element.49), channel_id=1, source_target_pairs={{0,128},{128,256},{256,384},{384,512},{512,640},{640,768},{768,896... | collective-permute-start | bytes 61448 | tf_op jit(solution)/shard_map/ppermute | solution.py:21
  90.4 1.9 %collective-permute-start.13 = (f32[1,8,5,128]{3,2,1,0:T(8,128)S(1)}, f32[1,8,5,128]{3,2,1,0:T(8,128)S(1)}, u32[]{:S(2)}, u32[]{:S(2)}) collective-permute-start(f32[1,8,5,128]{3,2,1,0:T(8,128)S(1)} %get-tuple-element.50), channel_id=1, source_target_pairs={{128,0},{256,128},{384,256},{512,384},{640,512},{768,640},{896,768... | collective-permute-start | bytes 61448 | tf_op jit(solution)/shard_map/ppermute | solution.py:24
  92.3 5.1 %collective-permute-done.13 = f32[1,8,5,128]{3,2,1,0:T(8,128)S(1)} collective-permute-done((f32[1,8,5,128]{3,2,1,0:T(8,128)S(1)}, f32[1,8,5,128]{3,2,1,0:T(8,128)S(1)}, u32[]{:S(2)}, u32[]{:S(2)}) %collective-permute-start.13) | collective-permute-done | bytes 20512 | tf_op jit(solution)/shard_map/ppermute | solution.py:24
  97.5 1.9 %collective-permute-start.14 = (f32[1,8,18,5]{3,2,1,0:T(8,128)S(1)}, f32[1,8,18,5]{3,2,1,0:T(8,128)S(1)}, u32[]{:S(2)}, u32[]{:S(2)}) collective-permute-start(f32[1,8,18,5]{3,2,1,0:T(8,128)S(1)} %get-tuple-element.41), channel_id=1, source_target_pairs={{0,2},{2,4},{4,6},{6,8},{8,10},{10,12},{12,14},{14,16},{16,18},{18... | collective-permute-start | bytes 8648 | tf_op jit(solution)/shard_map/ppermute | solution.py:21
  99.5 8.0 %collective-permute-start.15 = (f32[1,8,18,5]{3,2,1,0:T(8,128)S(1)}, f32[1,8,18,5]{3,2,1,0:T(8,128)S(1)}, u32[]{:S(2)}, u32[]{:S(2)}) collective-permute-start(f32[1,8,18,5]{3,2,1,0:T(8,128)S(1)} %get-tuple-element.42), channel_id=1, source_target_pairs={{2,0},{4,2},{6,4},{8,6},{10,8},{12,10},{14,12},{16,14},{18,16},{20... | collective-permute-start | bytes 8648 | tf_op jit(solution)/shard_map/ppermute | solution.py:24
  117.5 3.9 %collective-permute-start.16 = (f32[1,8,5,128]{3,2,1,0:T(8,128)S(1)}, f32[1,8,5,128]{3,2,1,0:T(8,128)S(1)}, u32[]{:S(2)}, u32[]{:S(2)}) collective-permute-start(f32[1,8,5,128]{3,2,1,0:T(8,128)S(1)} %get-tuple-element.47), channel_id=1, source_target_pairs={{0,128},{128,256},{256,384},{384,512},{512,640},{640,768},{768,896... | collective-permute-start | bytes 61448 | tf_op jit(solution)/shard_map/ppermute | solution.py:21
  121.4 1.9 %collective-permute-start.17 = (f32[1,8,5,128]{3,2,1,0:T(8,128)S(1)}, f32[1,8,5,128]{3,2,1,0:T(8,128)S(1)}, u32[]{:S(2)}, u32[]{:S(2)}) collective-permute-start(f32[1,8,5,128]{3,2,1,0:T(8,128)S(1)} %get-tuple-element.48), channel_id=1, source_target_pairs={{128,0},{256,128},{384,256},{512,384},{640,512},{768,640},{896,768... | collective-permute-start | bytes 61448 | tf_op jit(solution)/shard_map/ppermute | solution.py:24
  123.3 3.9 %collective-permute-done.17 = f32[1,8,5,128]{3,2,1,0:T(8,128)S(1)} collective-permute-done((f32[1,8,5,128]{3,2,1,0:T(8,128)S(1)}, f32[1,8,5,128]{3,2,1,0:T(8,128)S(1)}, u32[]{:S(2)}, u32[]{:S(2)}) %collective-permute-start.17) | collective-permute-done | bytes 20512 | tf_op jit(solution)/shard_map/ppermute | solution.py:24
  127.3 1.9 %collective-permute-start.18 = (f32[1,8,18,5]{3,2,1,0:T(8,128)S(1)}, f32[1,8,18,5]{3,2,1,0:T(8,128)S(1)}, u32[]{:S(2)}, u32[]{:S(2)}) collective-permute-start(f32[1,8,18,5]{3,2,1,0:T(8,128)S(1)} %get-tuple-element.39), channel_id=1, source_target_pairs={{0,2},{2,4},{4,6},{6,8},{8,10},{10,12},{12,14},{14,16},{16,18},{18... | collective-permute-start | bytes 8648 | tf_op jit(solution)/shard_map/ppermute | solution.py:21
  129.3 7.9 %collective-permute-start.19 = (f32[1,8,18,5]{3,2,1,0:T(8,128)S(1)}, f32[1,8,18,5]{3,2,1,0:T(8,128)S(1)}, u32[]{:S(2)}, u32[]{:S(2)}) collective-permute-start(f32[1,8,18,5]{3,2,1,0:T(8,128)S(1)} %get-tuple-element.40), channel_id=1, source_target_pairs={{2,0},{4,2},{6,4},{8,6},{10,8},{12,10},{14,12},{16,14},{18,16},{20... | collective-permute-start | bytes 8648 | tf_op jit(solution)/shard_map/ppermute | solution.py:24
  144.3 6.3 %all_to_all.12 = f32[1,8,8,128]{3,2,0,1:T(8,128)S(1)} all-to-all(f32[1,8,8,128]{3,2,0,1:T(8,128)S(1)} %fusion.20), channel_id=1, replica_groups=mesh['px'=8,'py'=64,'lev'=2] {'lev'}, dimensions={1} | all-to-all | bytes 65536 | tf_op jit(solution)/shard_map/all_to_all | solution.py:150
  (164 shorter events, 39.5 us)
Async XLA Ops:
  0.0 150.6 %copy-start = (f32[2,2]{1,0:T(2,128)S(1)}, f32[2,2]{1,0:T(2,128)}, u32[]{:S(2)}) copy-start(f32[2,2]{1,0:T(2,128)} %param.11) | copy-start | bytes 52
  0.0 39.8 %copy-start.1 = (f32[1,8,8,128]{3,2,1,0:T(8,128)S(1)}, f32[1,8,8,128]{3,2,1,0:T(8,128)}, u32[]{:S(2)}) copy-start(f32[1,8,8,128]{3,2,1,0:T(8,128)} %param.7) | copy-start | bytes 98308
  0.8 25.7 %collective-permute-start.8 = (f32[1,5,128]{2,1,0:T(8,128)S(1)}, f32[1,5,128]{2,1,0:T(8,128)S(1)}, u32[]{:S(2)}, u32[]{:S(2)}) collective-permute-start(f32[1,5,128]{2,1,0:T(8,128)S(1)} %get-tuple-element.67), channel_id=1, source_target_pairs={{0,128},{128,256},{256,384},{384,512},{512,640},{640,768},{768,896... | collective-permute-start | bytes 7688 | tf_op jit(solution)/shard_map/ppermute | solution.py:21
  4.4 22.1 %collective-permute-start.9 = (f32[1,5,128]{2,1,0:T(8,128)S(1)}, f32[1,5,128]{2,1,0:T(8,128)S(1)}, u32[]{:S(2)}, u32[]{:S(2)}) collective-permute-start(f32[1,5,128]{2,1,0:T(8,128)S(1)} %get-tuple-element.68), channel_id=1, source_target_pairs={{128,0},{256,128},{384,256},{512,384},{640,512},{768,640},{896,768... | collective-permute-start | bytes 7688 | tf_op jit(solution)/shard_map/ppermute | solution.py:24
  18.4 21.3 %collective-permute-start = (f32[1,8,4,128]{3,2,1,0:T(4,128)S(1)}, f32[1,8,4,128]{3,2,1,0:T(4,128)S(1)}, u32[]{:S(2)}, u32[]{:S(2)}) collective-permute-start(f32[1,8,4,128]{3,2,1,0:T(4,128)S(1)} %get-tuple-element.53), channel_id=1, source_target_pairs={{0,128},{128,256},{256,384},{384,512},{512,640},{640,768},{768,896... | collective-permute-start | bytes 49160 | tf_op jit(solution)/shard_map/ppermute | solution.py:21
  20.3 19.4 %collective-permute-start.1 = (f32[1,8,4,128]{3,2,1,0:T(4,128)S(1)}, f32[1,8,4,128]{3,2,1,0:T(4,128)S(1)}, u32[]{:S(2)}, u32[]{:S(2)}) collective-permute-start(f32[1,8,4,128]{3,2,1,0:T(4,128)S(1)} %get-tuple-element.54), channel_id=1, source_target_pairs={{128,0},{256,128},{384,256},{512,384},{640,512},{768,640},{896,768... | collective-permute-start | bytes 49160 | tf_op jit(solution)/shard_map/ppermute | solution.py:24
  27.2 9.8 %collective-permute-start.10 = (f32[1,18,5]{2,1,0:T(8,128)S(1)}, f32[1,18,5]{2,1,0:T(8,128)S(1)}, u32[]{:S(2)}, u32[]{:S(2)}) collective-permute-start(f32[1,18,5]{2,1,0:T(8,128)S(1)} %get-tuple-element.65), channel_id=1, source_target_pairs={{0,2},{2,4},{4,6},{6,8},{8,10},{10,12},{12,14},{14,16},{16,18},{18... | collective-permute-start | bytes 1088 | tf_op jit(solution)/shard_map/ppermute | solution.py:21
  29.2 9.3 %collective-permute-start.11 = (f32[1,18,5]{2,1,0:T(8,128)S(1)}, f32[1,18,5]{2,1,0:T(8,128)S(1)}, u32[]{:S(2)}, u32[]{:S(2)}) collective-permute-start(f32[1,18,5]{2,1,0:T(8,128)S(1)} %get-tuple-element.66), channel_id=1, source_target_pairs={{2,0},{4,2},{6,4},{8,6},{10,8},{12,10},{14,12},{16,14},{18,16},{20... | collective-permute-start | bytes 1088 | tf_op jit(solution)/shard_map/ppermute | solution.py:24
  39.9 10.3 %collective-permute-start.2 = (f32[1,8,16,4]{3,2,1,0:T(8,128)S(1)}, f32[1,8,16,4]{3,2,1,0:T(8,128)S(1)}, u32[]{:S(2)}, u32[]{:S(2)}) collective-permute-start(f32[1,8,16,4]{3,2,1,0:T(8,128)S(1)} %get-tuple-element.45), channel_id=1, source_target_pairs={{0,2},{2,4},{4,6},{6,8},{8,10},{10,12},{12,14},{14,16},{16,18},{18... | collective-permute-start | bytes 6152 | tf_op jit(solution)/shard_map/ppermute | solution.py:21
  41.8 10.3 %collective-permute-start.3 = (f32[1,8,16,4]{3,2,1,0:T(8,128)S(1)}, f32[1,8,16,4]{3,2,1,0:T(8,128)S(1)}, u32[]{:S(2)}, u32[]{:S(2)}) collective-permute-start(f32[1,8,16,4]{3,2,1,0:T(8,128)S(1)} %get-tuple-element.46), channel_id=1, source_target_pairs={{2,0},{4,2},{6,4},{8,6},{10,8},{12,10},{14,12},{16,14},{18,16},{20... | collective-permute-start | bytes 6152 | tf_op jit(solution)/shard_map/ppermute | solution.py:24
  54.6 7.4 %collective-permute-start.4 = (f32[1,8,5,128]{3,2,1,0:T(8,128)S(1)}, f32[1,8,5,128]{3,2,1,0:T(8,128)S(1)}, u32[]{:S(2)}, u32[]{:S(2)}) collective-permute-start(f32[1,8,5,128]{3,2,1,0:T(8,128)S(1)} %get-tuple-element.51), channel_id=1, source_target_pairs={{0,128},{128,256},{256,384},{384,512},{512,640},{640,768},{768,896... | collective-permute-start | bytes 61448 | tf_op jit(solution)/shard_map/ppermute | solution.py:21
  58.2 6.7 %collective-permute-start.5 = (f32[1,8,5,128]{3,2,1,0:T(8,128)S(1)}, f32[1,8,5,128]{3,2,1,0:T(8,128)S(1)}, u32[]{:S(2)}, u32[]{:S(2)}) collective-permute-start(f32[1,8,5,128]{3,2,1,0:T(8,128)S(1)} %get-tuple-element.52), channel_id=1, source_target_pairs={{128,0},{256,128},{384,256},{512,384},{640,512},{768,640},{896,768... | collective-permute-start | bytes 61448 | tf_op jit(solution)/shard_map/ppermute | solution.py:24
  65.1 10.2 %collective-permute-start.6 = (f32[1,8,18,5]{3,2,1,0:T(8,128)S(1)}, f32[1,8,18,5]{3,2,1,0:T(8,128)S(1)}, u32[]{:S(2)}, u32[]{:S(2)}) collective-permute-start(f32[1,8,18,5]{3,2,1,0:T(8,128)S(1)} %get-tuple-element.43), channel_id=1, source_target_pairs={{0,2},{2,4},{4,6},{6,8},{8,10},{10,12},{12,14},{14,16},{16,18},{18... | collective-permute-start | bytes 8648 | tf_op jit(solution)/shard_map/ppermute | solution.py:21
  67.0 10.6 %collective-permute-start.7 = (f32[1,8,18,5]{3,2,1,0:T(8,128)S(1)}, f32[1,8,18,5]{3,2,1,0:T(8,128)S(1)}, u32[]{:S(2)}, u32[]{:S(2)}) collective-permute-start(f32[1,8,18,5]{3,2,1,0:T(8,128)S(1)} %get-tuple-element.44), channel_id=1, source_target_pairs={{2,0},{4,2},{6,4},{8,6},{10,8},{12,10},{14,12},{16,14},{18,16},{20... | collective-permute-start | bytes 8648 | tf_op jit(solution)/shard_map/ppermute | solution.py:24
  82.3 1.0 copy-start.4
  82.3 1.0 copy-start.5
  85.5 6.8 %collective-permute-start.12 = (f32[1,8,5,128]{3,2,1,0:T(8,128)S(1)}, f32[1,8,5,128]{3,2,1,0:T(8,128)S(1)}, u32[]{:S(2)}, u32[]{:S(2)}) collective-permute-start(f32[1,8,5,128]{3,2,1,0:T(8,128)S(1)} %get-tuple-element.49), channel_id=1, source_target_pairs={{0,128},{128,256},{256,384},{384,512},{512,640},{640,768},{768,896... | collective-permute-start | bytes 61448 | tf_op jit(solution)/shard_map/ppermute | solution.py:21
  90.4 7.0 %collective-permute-start.13 = (f32[1,8,5,128]{3,2,1,0:T(8,128)S(1)}, f32[1,8,5,128]{3,2,1,0:T(8,128)S(1)}, u32[]{:S(2)}, u32[]{:S(2)}) collective-permute-start(f32[1,8,5,128]{3,2,1,0:T(8,128)S(1)} %get-tuple-element.50), channel_id=1, source_target_pairs={{128,0},{256,128},{384,256},{512,384},{640,512},{768,640},{896,768... | collective-permute-start | bytes 61448 | tf_op jit(solution)/shard_map/ppermute | solution.py:24
  97.5 10.2 %collective-permute-start.14 = (f32[1,8,18,5]{3,2,1,0:T(8,128)S(1)}, f32[1,8,18,5]{3,2,1,0:T(8,128)S(1)}, u32[]{:S(2)}, u32[]{:S(2)}) collective-permute-start(f32[1,8,18,5]{3,2,1,0:T(8,128)S(1)} %get-tuple-element.41), channel_id=1, source_target_pairs={{0,2},{2,4},{4,6},{6,8},{8,10},{10,12},{12,14},{14,16},{16,18},{18... | collective-permute-start | bytes 8648 | tf_op jit(solution)/shard_map/ppermute | solution.py:21
  99.5 10.1 %collective-permute-start.15 = (f32[1,8,18,5]{3,2,1,0:T(8,128)S(1)}, f32[1,8,18,5]{3,2,1,0:T(8,128)S(1)}, u32[]{:S(2)}, u32[]{:S(2)}) collective-permute-start(f32[1,8,18,5]{3,2,1,0:T(8,128)S(1)} %get-tuple-element.42), channel_id=1, source_target_pairs={{2,0},{4,2},{6,4},{8,6},{10,8},{12,10},{14,12},{16,14},{18,16},{20... | collective-permute-start | bytes 8648 | tf_op jit(solution)/shard_map/ppermute | solution.py:24
  117.5 5.9 %collective-permute-start.16 = (f32[1,8,5,128]{3,2,1,0:T(8,128)S(1)}, f32[1,8,5,128]{3,2,1,0:T(8,128)S(1)}, u32[]{:S(2)}, u32[]{:S(2)}) collective-permute-start(f32[1,8,5,128]{3,2,1,0:T(8,128)S(1)} %get-tuple-element.47), channel_id=1, source_target_pairs={{0,128},{128,256},{256,384},{384,512},{512,640},{640,768},{768,896... | collective-permute-start | bytes 61448 | tf_op jit(solution)/shard_map/ppermute | solution.py:21
  121.4 5.8 %collective-permute-start.17 = (f32[1,8,5,128]{3,2,1,0:T(8,128)S(1)}, f32[1,8,5,128]{3,2,1,0:T(8,128)S(1)}, u32[]{:S(2)}, u32[]{:S(2)}) collective-permute-start(f32[1,8,5,128]{3,2,1,0:T(8,128)S(1)} %get-tuple-element.48), channel_id=1, source_target_pairs={{128,0},{256,128},{384,256},{512,384},{640,512},{768,640},{896,768... | collective-permute-start | bytes 61448 | tf_op jit(solution)/shard_map/ppermute | solution.py:24
  127.3 10.2 %collective-permute-start.18 = (f32[1,8,18,5]{3,2,1,0:T(8,128)S(1)}, f32[1,8,18,5]{3,2,1,0:T(8,128)S(1)}, u32[]{:S(2)}, u32[]{:S(2)}) collective-permute-start(f32[1,8,18,5]{3,2,1,0:T(8,128)S(1)} %get-tuple-element.39), channel_id=1, source_target_pairs={{0,2},{2,4},{4,6},{6,8},{8,10},{10,12},{12,14},{14,16},{16,18},{18... | collective-permute-start | bytes 8648 | tf_op jit(solution)/shard_map/ppermute | solution.py:21
  129.3 10.1 %collective-permute-start.19 = (f32[1,8,18,5]{3,2,1,0:T(8,128)S(1)}, f32[1,8,18,5]{3,2,1,0:T(8,128)S(1)}, u32[]{:S(2)}, u32[]{:S(2)}) collective-permute-start(f32[1,8,18,5]{3,2,1,0:T(8,128)S(1)} %get-tuple-element.40), channel_id=1, source_target_pairs={{2,0},{4,2},{6,4},{8,6},{10,8},{12,10},{14,12},{16,14},{18,16},{20... | collective-permute-start | bytes 8648 | tf_op jit(solution)/shard_map/ppermute | solution.py:24
  (3 other events, 3.0 us)
where the time goes:
time: 152 us; the launch traced here: 151 us
  starting transfers between devices  92.4 us (61%)
  waiting for transfers between devices  21.8 us (14%)
  local copies, waits for them, and re-layouts  14.3 us (9%)
  other arithmetic  13.2 us (9%)
  blocking collectives  6.3 us (4%)
  matrix products  2.49 us (2%)
    ppermute x10, starting transfers between devices, extended(): lax.ppermute(lax.slice_in_dim(block, 0, width, axis=dim), axis, backward)  64.9 us
    ppermute x10, starting transfers between devices, extended(): lax.ppermute(lax.slice_in_dim(block, block.shape[dim] - width, None, axis...  27.4 us
    ppermute x10, waiting for transfers between devices, extended(): lax.ppermute(lax.slice_in_dim(block, 0, width, axis=dim), axis, backward)  21.2 us
    all_to_all x1, blocking collectives, shards(): lax.all_to_all(field, 'lev', split_axis=1, concat_axis=0, tiled=True)  6.3 us
    concatenate x8, other arithmetic, pair_sum(): jnp.concatenate([head_nodes + before, middle, tail_nodes + following], ax...  4.81 us
    add x8, other arithmetic, pair_sum(): head_nodes + before  3.66 us
  transfers between devices with their start and end apart: 20, of which 11 were waited for; matrix products, arithmetic and copies ran while one was open for 3% of the time, Pallas kernels for 0%

commit v1 on v0

v1 whole, which is shorter than its diff:
```python
import functools

import jax
import jax.numpy as jnp
import numpy as np
from jax import lax
from jax.experimental import pallas as pl
from jax.experimental.pallas import tpu as pltpu
from jax.sharding import PartitionSpec as P

GLL_NODES = 4
LANES = 128
PARAMS = pltpu.CompilerParams(vmem_limit_bytes=8 * 1024 * 1024)
SLOT = 32

sentinel = 1e30
step_size = 0.1
section_weights = ((0.0, 1.0), (0.75, 0.25), (1.0 / 3.0, 2.0 / 3.0))


def derivative_table():
    points = np.array([-1.0, -(5.0 ** (-0.5)), 5.0 ** (-0.5), 1.0])
    number = points.shape[0]
    barycentric = np.array(
        [
            1.0
            / np.prod([points[outer] - points[inner] for inner in range(number) if inner != outer])
            for outer in range(number)
        ]
    )
    table = np.zeros((number, number))
    for outer in range(number):
        for inner in range(number):
            if inner != outer:
                table[outer, inner] = (
                    barycentric[inner] / barycentric[outer] / (points[outer] - points[inner])
                )
    for outer in range(number):
        table[outer, outer] = -np.sum(table[outer])
    return table


def rot(x, k):
    k = k % LANES
    return pltpu.roll(x, k, 1) if k else x


def lane_index():
    return lax.broadcasted_iota(jnp.int32, (8, LANES), 1)


def edges_kernel(r_ref, in_ref, cross_ref):
    slot = lane_index() // SLOT
    even = lax.axis_index("py") % 2 == 0
    for r in range(8):
        left = right = None
        for a in range(4):
            x = r_ref[:, a, r, :]
            lo, hi = rot(x, SLOT * a), rot(x, SLOT * a + SLOT)
            left = lo if a == 0 else jnp.where(slot == a, lo, left)
            right = hi if a == 0 else jnp.where(slot == a, hi, right)
        in_ref[r] = jnp.where(even, right, left)
        cross_ref[r] = jnp.where(even, left, right)


def sections_kernel(r_ref, in_ref, cross_ref, out_ref):
    lane = lane_index()
    node = lane % GLL_NODES
    py = lax.axis_index("py")
    even = py % 2 == 0
    has_left = py > 0
    has_right = py < lax.axis_size("py") - 1
    exists = ((lane < 64) & has_right) | ((lane >= 64) & has_left)
    table = derivative_table() * step_size
    rows = range(8)

    def pairs(a, fill):
        own, halo = [], []
        for r in rows:
            from_right = jnp.where(even, in_ref[r], cross_ref[r])
            from_left = jnp.where(even, cross_ref[r], in_ref[r])
            second = jnp.where(
                lane >= LANES - SLOT, rot(from_left, -SLOT * a - SLOT), jnp.float32(fill)
            )
            second = jnp.where(lane < SLOT, rot(from_right, -SLOT * a), second)
            own.append(r_ref[:, a, r, :])
            halo.append(second)
        return [own, halo]

    def before(f, k):
        o, h = rot(f[0], k), rot(f[1], k)
        return jnp.where(lane < k, h, o), jnp.where(lane < k, o, h)

    def after(f, k):
        o, h = rot(f[0], -k), rot(f[1], -k)
        return jnp.where(lane >= LANES - k, h, o), jnp.where(lane >= LANES - k, o, h)

    def up(x):
        return pltpu.roll(x, 1, 0)

    def down(x):
        return pltpu.roll(x, 7, 0)

    def shared(f):
        f = [list(part) for part in f]
        for part in f:
            first, last = part[0], part[7]
            part[0] = first + up(last)
            part[7] = last + down(first)
            part[3] = part[4] = part[3] + part[4]
        for r in rows:
            both = (f[0][r], f[1][r])
            lo, hi = before(both, 1), after(both, 1)
            for s in range(2):
                extra = jnp.where(node == 0, lo[s], jnp.where(node == 3, hi[s], 0.0))
                f[s][r] = both[s] + extra
        return f

    def extreme(f, op, missing):
        parts = []
        for s in range(2):
            halves = []
            for e in range(2):
                x = f[s][4 * e]
                for i in range(1, 4):
                    x = op(x, f[s][4 * e + i])
                x = op(x, jnp.where(lane % 2 == 1, rot(x, 1), rot(x, -1)))
                x = op(x, jnp.where(node >= 2, rot(x, 2), rot(x, -2)))
                if s == 1:
                    x = jnp.where(exists, x, missing)
                halves.append(x)
            zero, one = halves
            parts.append((op(op(zero, one), up(one)), op(op(zero, one), down(zero))))
        result = [[None, None], [None, None]]
        for e in range(2):
            both = (parts[0][e], parts[1][e])
            lo, hi = before(both, 4), after(both, 4)
            for s in range(2):
                result[s][e] = op(op(both[s], lo[s]), hi[s])
        return result

    coefficient = {}
    for k in range(-3, 4):
        c = jnp.zeros((8, LANES), jnp.float32)
        for i in range(4):
            if 0 <= i + k < 4:
                c = jnp.where(node == i, jnp.float32(table[i, i + k]), c)
        coefficient[k] = c

    start = pairs(0, 0.0)
    mass = pairs(1, 1.0)
    wind_x = pairs(2, 0.0)
    wind_y = pairs(3, 0.0)
    mass_sum = shared(mass)
    inverse = [
        [1.0 / m for m in mass_sum[0]],
        [jnp.where(exists, 1.0 / jnp.where(exists, m, 1.0), 0.0) for m in mass_sum[1]],
    ]
    field = start
    for share_start, share_new in section_weights:
        lower = extreme(field, jnp.minimum, sentinel)
        upper = extreme(field, jnp.maximum, -sentinel)
        weighted = [[None] * 8, [None] * 8]
        for s in range(2):
            for e in range(2):
                flux_x = [wind_x[s][4 * e + i] * field[s][4 * e + i] for i in range(4)]
                for i in range(4):
                    r = 4 * e + i
                    slope = jnp.float32(table[i, 0]) * flux_x[0]
                    for j in range(1, 4):
                        slope = slope + jnp.float32(table[i, j]) * flux_x[j]
                    flux_y = wind_y[s][r] * field[s][r]
                    for k in range(-3, 4):
                        slope = slope + coefficient[k] * rot(flux_y, -k)
                    moved = field[s][r] - slope
                    limited = jnp.minimum(jnp.maximum(moved, lower[s][e]), upper[s][e])
                    weighted[s][r] = mass[s][r] * limited
        summed = shared(weighted)
        fresh = [[None] * 8, [None] * 8]
        for s in range(2):
            for r in rows:
                value = jnp.float32(share_new) * (summed[s][r] * inverse[s][r])
                if share_start:
                    value = jnp.float32(share_start) * start[s][r] + value
                fresh[s][r] = value
        field = fresh
    for r in rows:
        out_ref[:, 0, r, :] = field[0][r]
        out_ref[:, 1, r, :] = field[0][r]


def remap_kernel(remap_ref, x_ref, out_ref):
    base = lax.axis_index("lev") * 8
    for t in range(4):
        low, high = x_ref[base + 2 * t], x_ref[base + 2 * t + 1]
        for level in range(2):
            out_ref[level, t] = remap_ref[level, 0] * low + remap_ref[level, 1] * high


def vmem(count):
    return [pl.BlockSpec(memory_space=pltpu.VMEM)] * count


def shards(tracer, node_mass, wind_x, wind_y, remap):
    count = lax.axis_size("py")
    common = jnp.stack([node_mass[0], wind_x[0], wind_y[0]])
    packed = jnp.concatenate(
        [tracer[0][:, None], jnp.broadcast_to(common[None], (8, 3, 8, LANES))], axis=1
    )
    rows = lax.all_to_all(packed, "px", 0, 0, tiled=True)
    edge = jax.ShapeDtypeStruct((8, 8, LANES), jnp.float32)
    inside, cross = pl.pallas_call(
        edges_kernel,
        out_shape=(edge, edge),
        in_specs=vmem(1),
        out_specs=tuple(vmem(2)),
        compiler_params=PARAMS,
        name="edges",
    )(rows)
    cross_pairs = [(i, i + 1 if i % 2 else i - 1) for i in range(1, count - 1)]
    inside_pairs = [(i, i ^ 1) for i in range(count)]
    cross = lax.ppermute(cross, "py", cross_pairs)
    inside = lax.ppermute(inside, "py", inside_pairs)
    done = pl.pallas_call(
        sections_kernel,
        out_shape=jax.ShapeDtypeStruct((8, 2, 8, LANES), jnp.float32),
        in_specs=vmem(3),
        out_specs=vmem(1)[0],
        compiler_params=PARAMS,
        name="sections",
    )(rows, inside, cross)
    back = lax.all_to_all(done.reshape(16, 8, LANES), ("px", "lev"), 0, 0, tiled=True)
    return pl.pallas_call(
        remap_kernel,
        out_shape=jax.ShapeDtypeStruct((2, 4, 8, LANES), jnp.float32),
        in_specs=[pl.BlockSpec(memory_space=pltpu.SMEM)] + vmem(1),
        out_specs=vmem(1)[0],
        compiler_params=PARAMS,
        name="remap",
    )(remap, back)


def solution(mesh):
    in_specs = (
        P("lev", None, "px", "py"),
        P("lev", "px", "py"),
        P("lev", "px", "py"),
        P("lev", "px", "py"),
        P(),
    )
    out_specs = P(None, "lev", "px", "py")
    return jax.shard_map(shards, mesh=mesh, in_specs=in_specs, out_specs=out_specs, check_vma=False)
```

time: 152 us -> 55.8 us (0.37)
  the two profiles are of different devices: /device:TPU:16 before, /device:TPU:14 now
where the time goes in v1:
time: 55.8 us; the launch traced here: 55.5 us
  blocking collectives  28.5 us (51%)
  starting transfers between devices  21.1 us (38%)
  Pallas kernels  2.85 us (5%)
  waiting for transfers between devices  1.58 us (3%)
  local copies, waits for them, and re-layouts  0.76 us (1%)
  other arithmetic  0.73 us (1%)
    ppermute x1, starting transfers between devices, shards(): cross = lax.ppermute(cross, 'py', cross_pairs)  19.1 us
    all_to_all x1, blocking collectives, shards(): rows = lax.all_to_all(packed, 'px', 0, 0, tiled=True)  16.5 us
    all_to_all x1, blocking collectives, shards(): lax.all_to_all(done.reshape(16, 8, LANES), ('px', 'lev'), 0, 0, tiled=True)  12 us
    ppermute x1, starting transfers between devices, shards(): inside = lax.ppermute(inside, 'py', inside_pairs)  1.92 us
    ppermute x1, waiting for transfers between devices, shards(): cross = lax.ppermute(cross, 'py', cross_pairs)  1.57 us
    pallas_call x1, Pallas kernels, shards(): pl.pallas_call(sections_kernel, out_shape=jax.ShapeDtypeStruct((8, 2, 8,...  1.54 us
    pallas_call x1, Pallas kernels, shards(): pl.pallas_call(remap_kernel, out_shape=jax.ShapeDtypeStruct((2, 4, 8, LAN...  1.18 us
  transfers between devices with their start and end apart: 2, of which 1 were waited for; matrix products, arithmetic and copies ran while one was open for 0% of the time, Pallas kernels for 0%

profile of v1, /device:TPU:14, one launch (start us, length us, event | category | flops | bytes accessed | tf_op | source)
XLA Modules:
  0.0 55.5 jit_solution(15203967064077620147)
XLA Ops:
  0.0 0.7 %pad_maximum_fusion.1 = f32[3,8,128]{2,1,0:T(8,128)S(1)} fusion(f32[1,8,128]{2,1,0:T(8,128)} %param.8, f32[1,8,128]{2,1,0:T(8,128)} %param.7, f32[1,8,128]{2,1,0:T(8,128)} %param.6), kind=kLoop, calls=%fused_computation.1 | loop fusion | flops 6144 | bytes 24576 | tf_op jit(solution)/shard_map/stack | solution.py:206
  0.7 0.0 copy-start.1
  0.7 0.7 %copy-done.1 = f32[1,8,8,128]{3,2,1,0:T(8,128)S(1)} copy-done((f32[1,8,8,128]{3,2,1,0:T(8,128)S(1)}, f32[1,8,8,128]{3,2,1,0:T(8,128)}, u32[]{:S(2)}) %copy-start.1) | copy-done | bytes 32792
  1.5 16.5 %all_to_all.10.r_ref = f32[8,4,8,128]{3,2,1,0:T(8,128)S(1)} all-to-all(f32[8,4,8,128]{3,2,1,0:T(8,128)S(1)} %pad_maximum_fusion), channel_id=1, replica_groups=mesh['px'=8,'py'=64,'lev'=2] {'px'}, dimensions={0} | all-to-all | bytes 262144 | tf_op jit(solution)/shard_map/all_to_all | solution.py:210
  18.0 0.1 edges.1
  18.1 1.9 %collective-permute-start = (f32[8,8,128]{2,1,0:T(8,128)S(1)}, f32[8,8,128]{2,1,0:T(8,128)S(1)}, u32[]{:S(2)}, u32[]{:S(2)}) collective-permute-start(f32[8,8,128]{2,1,0:T(8,128)S(1)} %get-tuple-element.7), channel_id=1, source_target_pairs={{0,2},{2,0},{4,6},{6,4},{8,10},{10,8},{12,14},{14,12},{16,18},{18,... | collective-permute-start | bytes 98312 | tf_op jit(solution)/shard_map/ppermute | solution.py:223
  20.0 19.1 %collective-permute-start.1 = (f32[8,8,128]{2,1,0:T(8,128)S(1)}, f32[8,8,128]{2,1,0:T(8,128)S(1)}, u32[]{:S(2)}, u32[]{:S(2)}) collective-permute-start(f32[8,8,128]{2,1,0:T(8,128)S(1)} %get-tuple-element.8), channel_id=1, source_target_pairs={{2,4},{4,2},{6,8},{8,6},{10,12},{12,10},{14,16},{16,14},{18,20},{2... | collective-permute-start | bytes 98312 | tf_op jit(solution)/shard_map/ppermute | solution.py:222
  39.2 0.0 collective-permute-done.in_ref
  39.2 1.6 %collective-permute-done.1.cross_ref = f32[8,8,128]{2,1,0:T(8,128)S(1)} collective-permute-done((f32[8,8,128]{2,1,0:T(8,128)S(1)}, f32[8,8,128]{2,1,0:T(8,128)S(1)}, u32[]{:S(2)}, u32[]{:S(2)}) %collective-permute-start.1) | collective-permute-done | bytes 32800 | tf_op jit(solution)/shard_map/ppermute | solution.py:222
  40.8 1.5 %sections.1 = f32[8,2,8,128]{3,2,1,0:T(8,128)S(1)} custom-call(f32[8,4,8,128]{3,2,1,0:T(8,128)S(1)} %all_to_all.10.r_ref, f32[8,8,128]{2,1,0:T(8,128)S(1)} %collective-permute-done.in_ref, f32[8,8,128]{2,1,0:T(8,128)S(1)} %collective-permute-done.1.cross_ref), custom_call_target="tpu_custom_call" | custom-call | tf_op jit(solution)/shard_map/sections/pallas_call | solution.py:224
  42.3 0.0 copy-start
  42.3 12.0 %all_to_all.11.x_ref = f32[16,8,128]{2,1,0:T(8,128)S(1)} all-to-all(f32[16,8,128]{2,1,0:T(8,128)S(1)} %bitcast.2), channel_id=1, replica_groups=mesh['px'=8,'py'=64,'lev'=2] {'px','lev'}, dimensions={0} | all-to-all | bytes 131072 | tf_op jit(solution)/shard_map/all_to_all | solution.py:232
  54.3 0.0 copy-done
  54.3 1.2 %remap.1 = f32[2,4,8,128]{3,2,1,0:T(8,128)} custom-call(f32[2,2]{1,0:T(2,128)S(1)} %copy-done, f32[16,8,128]{2,1,0:T(8,128)S(1)} %all_to_all.11.x_ref), custom_call_target="tpu_custom_call" | custom-call | tf_op jit(solution)/shard_map/remap/pallas_call | solution.py:233
  (2 shorter events, 0.0 us)
Async XLA Ops:
  0.7 0.8 %copy-start.1 = (f32[1,8,8,128]{3,2,1,0:T(8,128)S(1)}, f32[1,8,8,128]{3,2,1,0:T(8,128)}, u32[]{:S(2)}) copy-start(f32[1,8,8,128]{3,2,1,0:T(8,128)} %param.5) | copy-start | bytes 98308
  18.1 21.1 %collective-permute-start = (f32[8,8,128]{2,1,0:T(8,128)S(1)}, f32[8,8,128]{2,1,0:T(8,128)S(1)}, u32[]{:S(2)}, u32[]{:S(2)}) collective-permute-start(f32[8,8,128]{2,1,0:T(8,128)S(1)} %get-tuple-element.7), channel_id=1, source_target_pairs={{0,2},{2,0},{4,6},{6,4},{8,10},{10,8},{12,14},{14,12},{16,18},{18,... | collective-permute-start | bytes 98312 | tf_op jit(solution)/shard_map/ppermute | solution.py:223
  20.0 20.7 %collective-permute-start.1 = (f32[8,8,128]{2,1,0:T(8,128)S(1)}, f32[8,8,128]{2,1,0:T(8,128)S(1)}, u32[]{:S(2)}, u32[]{:S(2)}) collective-permute-start(f32[8,8,128]{2,1,0:T(8,128)S(1)} %get-tuple-element.8), channel_id=1, source_target_pairs={{2,4},{4,2},{6,8},{8,6},{10,12},{12,10},{14,16},{16,14},{18,20},{2... | collective-permute-start | bytes 98312 | tf_op jit(solution)/shard_map/ppermute | solution.py:222
  42.3 12.0 %copy-start = (f32[2,2]{1,0:T(2,128)S(1)}, f32[2,2]{1,0:T(2,128)}, u32[]{:S(2)}) copy-start(f32[2,2]{1,0:T(2,128)} %remap_ref.1) | copy-start | bytes 52

commit v2 on v1

--- a/solution.py
+++ b/solution.py
@@ -1,5 +1,3 @@
-import functools
-
 import jax
 import jax.numpy as jnp
 import numpy as np
@@ -7,6 +5,7 @@
 from jax.experimental import pallas as pl
 from jax.experimental.pallas import tpu as pltpu
 from jax.sharding import PartitionSpec as P
+
 
 GLL_NODES = 4
 LANES = 128
@@ -191,21 +190,24 @@
 
 def remap_kernel(remap_ref, x_ref, out_ref):
     base = lax.axis_index("lev") * 8
+    weight = [[remap_ref[a : a + 1, b : b + 1] for b in range(2)] for a in range(2)]
     for t in range(4):
         low, high = x_ref[base + 2 * t], x_ref[base + 2 * t + 1]
-        for level in range(2):
-            out_ref[level, t] = remap_ref[level, 0] * low + remap_ref[level, 1] * high
+        for a in range(2):
+            out_ref[a, t] = weight[a][0] * low + weight[a][1] * high
 
 
 def vmem(count):
     return [pl.BlockSpec(memory_space=pltpu.VMEM)] * count
 
 
-def shards(tracer, node_mass, wind_x, wind_y, remap):
+def step(tracer, node_mass, wind_x, wind_y, remap):
     count = lax.axis_size("py")
-    common = jnp.stack([node_mass[0], wind_x[0], wind_y[0]])
+    whole = (8, 1, 8, LANES)
     packed = jnp.concatenate(
-        [tracer[0][:, None], jnp.broadcast_to(common[None], (8, 3, 8, LANES))], axis=1
+        [tracer.reshape(whole)]
+        + [jnp.broadcast_to(part[None], whole) for part in (node_mass, wind_x, wind_y)],
+        axis=1,
     )
     rows = lax.all_to_all(packed, "px", 0, 0, tiled=True)
     edge = jax.ShapeDtypeStruct((8, 8, LANES), jnp.float32)
@@ -233,7 +235,7 @@
     return pl.pallas_call(
         remap_kernel,
         out_shape=jax.ShapeDtypeStruct((2, 4, 8, LANES), jnp.float32),
-        in_specs=[pl.BlockSpec(memory_space=pltpu.SMEM)] + vmem(1),
+        in_specs=vmem(2),
         out_specs=vmem(1)[0],
         compiler_params=PARAMS,
         name="remap",
@@ -249,4 +251,6 @@
         P(),
     )
     out_specs = P(None, "lev", "px", "py")
-    return jax.shard_map(shards, mesh=mesh, in_specs=in_specs, out_specs=out_specs, check_vma=False)
+    return jax.shard_map(
+        step, mesh=mesh, in_specs=in_specs, out_specs=out_specs, check_vma=False
+    )

time: 55.8 us -> 55.4 us (level)
  other arithmetic: 0.73 us -> 0.01 us
  local copies, waits for them, and re-layouts: 0.76 us -> 1.47 us
    another operation x1 -> x0, other arithmetic: 0.72 us -> none  [shards(): common = jnp.stack([node_mass[0], wind_x[0], wind_y[0]])]
    broadcast_in_dim x1 -> x3, local copies, waits for them, and re-layouts: 0.01 us -> 0.71 us  [step(): jnp.broadcast_to(part[None], whole)]
where the time goes in v2:
time: 55.4 us; the launch traced here: 55 us
  blocking collectives  28.5 us (51%)
  starting transfers between devices  21.1 us (38%)
  Pallas kernels  2.4 us (4%)
  waiting for transfers between devices  1.58 us (3%)
  local copies, waits for them, and re-layouts  1.47 us (3%)
    ppermute x1, starting transfers between devices, step(): cross = lax.ppermute(cross, 'py', cross_pairs)  19.1 us
    all_to_all x1, blocking collectives, step(): rows = lax.all_to_all(packed, 'px', 0, 0, tiled=True)  16.5 us
    all_to_all x1, blocking collectives, step(): lax.all_to_all(done.reshape(16, 8, LANES), ('px', 'lev'), 0, 0, tiled=True)  12 us
    ppermute x1, starting transfers between devices, step(): inside = lax.ppermute(inside, 'py', inside_pairs)  1.92 us
    ppermute x1, waiting for transfers between devices, step(): cross = lax.ppermute(cross, 'py', cross_pairs)  1.57 us
    pallas_call x1, Pallas kernels, step(): pl.pallas_call(sections_kernel, out_shape=jax.ShapeDtypeStruct((8, 2, 8,...  1.54 us
  transfers between devices with their start and end apart: 2, of which 1 were waited for; matrix products, arithmetic and copies ran while one was open for 0% of the time, Pallas kernels for 0%

profile of v2, /device:TPU:14, one launch (start us, length us, event | category | flops | bytes accessed | tf_op | source)
XLA Modules:
  0.0 55.0 jit_solution(15921581773292837585)
XLA Ops:
  0.0 0.0 copy-start.2
  0.0 0.7 %broadcast_in_dim.25 = f32[8,1,8,128]{3,2,1,0:T(8,128)S(1)} broadcast(f32[8,128]{1,0:T(8,128)} %bitcast.7), dimensions={2,3} | broadcast | bytes 36864 | tf_op jit(solution)/shard_map/broadcast_in_dim | solution.py:209
  0.7 0.0 copy-done.2
  0.7 0.0 copy-start.3
  0.7 0.0 copy-start.1
  0.7 0.7 %copy-done.3 = f32[1,8,128]{2,1,0:T(8,128)S(1)} copy-done((f32[1,8,128]{2,1,0:T(8,128)S(1)}, f32[1,8,128]{2,1,0:T(8,128)}, u32[]{:S(2)}) %copy-start.3) | copy-done | bytes 4120
  1.4 0.1 copy-done.1
  1.5 16.5 %all_to_all.10.r_ref = f32[8,4,8,128]{3,2,1,0:T(8,128)S(1)} all-to-all(f32[8,4,8,128]{3,2,1,0:T(8,128)S(1)} %pad_maximum_fusion), channel_id=1, replica_groups=mesh['px'=8,'py'=64,'lev'=2] {'px'}, dimensions={0} | all-to-all | bytes 262144 | tf_op jit(solution)/shard_map/all_to_all | solution.py:212
  18.0 0.1 edges.1
  18.1 1.9 %collective-permute-start = (f32[8,8,128]{2,1,0:T(8,128)S(1)}, f32[8,8,128]{2,1,0:T(8,128)S(1)}, u32[]{:S(2)}, u32[]{:S(2)}) collective-permute-start(f32[8,8,128]{2,1,0:T(8,128)S(1)} %get-tuple-element.7), channel_id=1, source_target_pairs={{0,2},{2,0},{4,6},{6,4},{8,10},{10,8},{12,14},{14,12},{16,18},{18,... | collective-permute-start | bytes 98312 | tf_op jit(solution)/shard_map/ppermute | solution.py:225
  20.0 19.1 %collective-permute-start.1 = (f32[8,8,128]{2,1,0:T(8,128)S(1)}, f32[8,8,128]{2,1,0:T(8,128)S(1)}, u32[]{:S(2)}, u32[]{:S(2)}) collective-permute-start(f32[8,8,128]{2,1,0:T(8,128)S(1)} %get-tuple-element.8), channel_id=1, source_target_pairs={{2,4},{4,2},{6,8},{8,6},{10,12},{12,10},{14,16},{16,14},{18,20},{2... | collective-permute-start | bytes 98312 | tf_op jit(solution)/shard_map/ppermute | solution.py:224
  39.2 0.0 collective-permute-done.in_ref
  39.2 1.6 %collective-permute-done.1.cross_ref = f32[8,8,128]{2,1,0:T(8,128)S(1)} collective-permute-done((f32[8,8,128]{2,1,0:T(8,128)S(1)}, f32[8,8,128]{2,1,0:T(8,128)S(1)}, u32[]{:S(2)}, u32[]{:S(2)}) %collective-permute-start.1) | collective-permute-done | bytes 32800 | tf_op jit(solution)/shard_map/ppermute | solution.py:224
  40.8 1.5 %sections.1 = f32[8,2,8,128]{3,2,1,0:T(8,128)S(1)} custom-call(f32[8,4,8,128]{3,2,1,0:T(8,128)S(1)} %all_to_all.10.r_ref, f32[8,8,128]{2,1,0:T(8,128)S(1)} %collective-permute-done.in_ref, f32[8,8,128]{2,1,0:T(8,128)S(1)} %collective-permute-done.1.cross_ref), custom_call_target="tpu_custom_call" | custom-call | tf_op jit(solution)/shard_map/sections/pallas_call | solution.py:226
  42.3 0.0 copy-start
  42.3 12.0 %all_to_all.11.x_ref = f32[16,8,128]{2,1,0:T(8,128)S(1)} all-to-all(f32[16,8,128]{2,1,0:T(8,128)S(1)} %bitcast.5), channel_id=1, replica_groups=mesh['px'=8,'py'=64,'lev'=2] {'px','lev'}, dimensions={0} | all-to-all | bytes 131072 | tf_op jit(solution)/shard_map/all_to_all | solution.py:234
  54.3 0.0 copy-done
  54.3 0.7 %remap.1 = f32[2,4,8,128]{3,2,1,0:T(8,128)} custom-call(f32[2,2]{1,0:T(2,128)S(1)} %copy-done, f32[16,8,128]{2,1,0:T(8,128)S(1)} %all_to_all.11.x_ref), custom_call_target="tpu_custom_call" | custom-call | tf_op jit(solution)/shard_map/remap/pallas_call | solution.py:235
  (3 shorter events, 0.0 us)
Async XLA Ops:
  0.0 0.7 %copy-start.2 = (f32[1,8,128]{2,1,0:T(8,128)S(1)}, f32[1,8,128]{2,1,0:T(8,128)}, u32[]{:S(2)}) copy-start(f32[1,8,128]{2,1,0:T(8,128)} %param.7) | copy-start | bytes 12292
  0.7 0.7 %copy-start.3 = (f32[1,8,128]{2,1,0:T(8,128)S(1)}, f32[1,8,128]{2,1,0:T(8,128)}, u32[]{:S(2)}) copy-start(f32[1,8,128]{2,1,0:T(8,128)} %param.8) | copy-start | bytes 12292
  0.7 0.8 %copy-start.1 = (f32[1,8,8,128]{3,2,1,0:T(8,128)S(1)}, f32[1,8,8,128]{3,2,1,0:T(8,128)}, u32[]{:S(2)}) copy-start(f32[1,8,8,128]{3,2,1,0:T(8,128)} %param.5) | copy-start | bytes 98308
  18.1 21.1 %collective-permute-start = (f32[8,8,128]{2,1,0:T(8,128)S(1)}, f32[8,8,128]{2,1,0:T(8,128)S(1)}, u32[]{:S(2)}, u32[]{:S(2)}) collective-permute-start(f32[8,8,128]{2,1,0:T(8,128)S(1)} %get-tuple-element.7), channel_id=1, source_target_pairs={{0,2},{2,0},{4,6},{6,4},{8,10},{10,8},{12,14},{14,12},{16,18},{18,... | collective-permute-start | bytes 98312 | tf_op jit(solution)/shard_map/ppermute | solution.py:225
  20.0 20.7 %collective-permute-start.1 = (f32[8,8,128]{2,1,0:T(8,128)S(1)}, f32[8,8,128]{2,1,0:T(8,128)S(1)}, u32[]{:S(2)}, u32[]{:S(2)}) collective-permute-start(f32[8,8,128]{2,1,0:T(8,128)S(1)} %get-tuple-element.8), channel_id=1, source_target_pairs={{2,4},{4,2},{6,8},{8,6},{10,12},{12,10},{14,16},{16,14},{18,20},{2... | collective-permute-start | bytes 98312 | tf_op jit(solution)/shard_map/ppermute | solution.py:224
  42.3 12.0 %copy-start = (f32[2,2]{1,0:T(2,128)S(1)}, f32[2,2]{1,0:T(2,128)}, u32[]{:S(2)}) copy-start(f32[2,2]{1,0:T(2,128)} %remap_ref.1) | copy-start | bytes 52

commit v3 on v2

--- a/solution.py
+++ b/solution.py
@@ -48,13 +48,39 @@
     return lax.broadcasted_iota(jnp.int32, (8, LANES), 1)
 
 
+def node_index():
+    return lane_index() % GLL_NODES
+
+
+def table_kernel(out_ref):
+    table = derivative_table() * step_size
+    node = node_index()
+    for m in range(4):
+        c = jnp.full((8, LANES), table[0, m], jnp.float32)
+        for i in range(1, 4):
+            c = jnp.where(node == i, jnp.float32(table[i, i ^ m]), c)
+        out_ref[m] = c
+
+
+def pack_kernel(first_ref, t_ref, m_ref, x_ref, y_ref, out_ref):
+    common = [ref[0] for ref in (m_ref, x_ref, y_ref)]
+    for i in range(8):
+        out_ref[i, 0] = t_ref[0, i]
+        for a in range(3):
+            out_ref[i, a + 1] = common[a]
+
+
+def gathered(r_ref, a, r):
+    return r_ref[pl.ds(a * 8 + r, 8, stride=32), :]
+
+
 def edges_kernel(r_ref, in_ref, cross_ref):
     slot = lane_index() // SLOT
     even = lax.axis_index("py") % 2 == 0
     for r in range(8):
         left = right = None
         for a in range(4):
-            x = r_ref[:, a, r, :]
+            x = gathered(r_ref, a, r)
             lo, hi = rot(x, SLOT * a), rot(x, SLOT * a + SLOT)
             left = lo if a == 0 else jnp.where(slot == a, lo, left)
             right = hi if a == 0 else jnp.where(slot == a, hi, right)
@@ -62,16 +88,23 @@
         cross_ref[r] = jnp.where(even, left, right)
 
 
-def sections_kernel(r_ref, in_ref, cross_ref, out_ref):
+def sections_kernel(r_ref, in_ref, cross_ref, table_ref, out_ref):
     lane = lane_index()
-    node = lane % GLL_NODES
+    node = node_index()
     py = lax.axis_index("py")
     even = py % 2 == 0
     has_left = py > 0
     has_right = py < lax.axis_size("py") - 1
     exists = ((lane < 64) & has_right) | ((lane >= 64) & has_left)
+    rim_node = (node == 0) | (node == 3)
+    rim_lane = (lane == 0) | (lane == LANES - 1)
+    partner = jnp.where(node == 0, lane - 1, jnp.where(node == 3, lane + 1, lane))
+    partner = (partner + LANES) % LANES
     table = derivative_table() * step_size
     rows = range(8)
+
+    def permuted(x, index):
+        return jnp.take_along_axis(x, index, axis=1, mode="promise_in_bounds")
 
     def pairs(a, fill):
         own, halo = [], []
@@ -82,7 +115,7 @@
                 lane >= LANES - SLOT, rot(from_left, -SLOT * a - SLOT), jnp.float32(fill)
             )
             second = jnp.where(lane < SLOT, rot(from_right, -SLOT * a), second)
-            own.append(r_ref[:, a, r, :])
+            own.append(gathered(r_ref, a, r))
             halo.append(second)
         return [own, halo]
 
@@ -108,11 +141,10 @@
             part[7] = last + down(first)
             part[3] = part[4] = part[3] + part[4]
         for r in rows:
-            both = (f[0][r], f[1][r])
-            lo, hi = before(both, 1), after(both, 1)
-            for s in range(2):
-                extra = jnp.where(node == 0, lo[s], jnp.where(node == 3, hi[s], 0.0))
-                f[s][r] = both[s] + extra
+            own, halo = f[0][r], f[1][r]
+            o, h = permuted(own, partner), permuted(halo, partner)
+            f[0][r] = own + jnp.where(rim_node, jnp.where(rim_lane, h, o), 0.0)
+            f[1][r] = halo + jnp.where(rim_node, jnp.where(rim_lane, o, h), 0.0)
         return f
 
     def extreme(f, op, missing):
@@ -120,16 +152,15 @@
         for s in range(2):
             halves = []
             for e in range(2):
-                x = f[s][4 * e]
-                for i in range(1, 4):
-                    x = op(x, f[s][4 * e + i])
-                x = op(x, jnp.where(lane % 2 == 1, rot(x, 1), rot(x, -1)))
-                x = op(x, jnp.where(node >= 2, rot(x, 2), rot(x, -2)))
+                x = op(op(f[s][4 * e], f[s][4 * e + 1]), op(f[s][4 * e + 2], f[s][4 * e + 3]))
+                x = op(x, permuted(x, lane ^ 1))
+                x = op(x, permuted(x, lane ^ 2))
                 if s == 1:
                     x = jnp.where(exists, x, missing)
                 halves.append(x)
             zero, one = halves
-            parts.append((op(op(zero, one), up(one)), op(op(zero, one), down(zero))))
+            both = op(zero, one)
+            parts.append((op(both, up(one)), op(both, down(zero))))
         result = [[None, None], [None, None]]
         for e in range(2):
             both = (parts[0][e], parts[1][e])
@@ -138,18 +169,22 @@
                 result[s][e] = op(op(both[s], lo[s]), hi[s])
         return result
 
-    coefficient = {}
-    for k in range(-3, 4):
-        c = jnp.zeros((8, LANES), jnp.float32)
-        for i in range(4):
-            if 0 <= i + k < 4:
-                c = jnp.where(node == i, jnp.float32(table[i, i + k]), c)
-        coefficient[k] = c
+    def slopes_x(f):
+        outer, inner = f[0] - f[3], f[1] - f[2]
+        even_part = (f[0] + f[3]) - (f[1] + f[2])
+        result = [None] * 4
+        for i in range(2):
+            p = jnp.float32((table[i, 0] - table[i, 3]) / 2) * outer
+            p = p + jnp.float32((table[i, 1] - table[i, 2]) / 2) * inner
+            q = jnp.float32((table[i, 0] + table[i, 3]) / 2) * even_part
+            result[i], result[3 - i] = p + q, p - q
+        return result
 
     start = pairs(0, 0.0)
     mass = pairs(1, 1.0)
     wind_x = pairs(2, 0.0)
     wind_y = pairs(3, 0.0)
+    coefficient = [table_ref[m] for m in range(4)]
     mass_sum = shared(mass)
     inverse = [
         [1.0 / m for m in mass_sum[0]],
@@ -162,15 +197,13 @@
         weighted = [[None] * 8, [None] * 8]
         for s in range(2):
             for e in range(2):
-                flux_x = [wind_x[s][4 * e + i] * field[s][4 * e + i] for i in range(4)]
+                along_x = slopes_x([wind_x[s][4 * e + i] * field[s][4 * e + i] for i in range(4)])
                 for i in range(4):
                     r = 4 * e + i
-                    slope = jnp.float32(table[i, 0]) * flux_x[0]
-                    for j in range(1, 4):
-                        slope = slope + jnp.float32(table[i, j]) * flux_x[j]
                     flux_y = wind_y[s][r] * field[s][r]
-                    for k in range(-3, 4):
-                        slope = slope + coefficient[k] * rot(flux_y, -k)
+                    slope = along_x[i] + coefficient[0] * flux_y
+                    for m in range(1, 4):
+                        slope = slope + coefficient[m] * permuted(flux_y, lane ^ m)
                     moved = field[s][r] - slope
                     limited = jnp.minimum(jnp.maximum(moved, lower[s][e]), upper[s][e])
                     weighted[s][r] = mass[s][r] * limited
@@ -178,14 +211,16 @@
         fresh = [[None] * 8, [None] * 8]
         for s in range(2):
             for r in rows:
-                value = jnp.float32(share_new) * (summed[s][r] * inverse[s][r])
+                value = summed[s][r] * inverse[s][r]
+                if share_new != 1.0:
+                    value = jnp.float32(share_new) * value
                 if share_start:
                     value = jnp.float32(share_start) * start[s][r] + value
                 fresh[s][r] = value
         field = fresh
     for r in rows:
-        out_ref[:, 0, r, :] = field[0][r]
-        out_ref[:, 1, r, :] = field[0][r]
+        for m in range(2):
+            out_ref[pl.ds(m * 8 + r, 8, stride=16), :] = field[0][r]
 
 
 def remap_kernel(remap_ref, x_ref, out_ref):
@@ -203,13 +238,23 @@
 
 def step(tracer, node_mass, wind_x, wind_y, remap):
     count = lax.axis_size("py")
-    whole = (8, 1, 8, LANES)
-    packed = jnp.concatenate(
-        [tracer.reshape(whole)]
-        + [jnp.broadcast_to(part[None], whole) for part in (node_mass, wind_x, wind_y)],
-        axis=1,
-    )
-    rows = lax.all_to_all(packed, "px", 0, 0, tiled=True)
+    tables = pl.pallas_call(
+        table_kernel,
+        out_shape=jax.ShapeDtypeStruct((4, 8, LANES), jnp.float32),
+        out_specs=vmem(1)[0],
+        compiler_params=PARAMS,
+        cost_estimate=pl.CostEstimate(flops=10**10, bytes_accessed=10**7, transcendentals=0),
+        name="tables",
+    )()
+    packed = pl.pallas_call(
+        pack_kernel,
+        out_shape=jax.ShapeDtypeStruct((8, 4, 8, LANES), jnp.float32),
+        in_specs=vmem(5),
+        out_specs=vmem(1)[0],
+        compiler_params=PARAMS,
+        name="pack",
+    )(tables, tracer, node_mass, wind_x, wind_y)
+    rows = lax.all_to_all(packed, "px", 0, 0, tiled=True).reshape(256, LANES)
     edge = jax.ShapeDtypeStruct((8, 8, LANES), jnp.float32)
     inside, cross = pl.pallas_call(
         edges_kernel,
@@ -225,12 +270,12 @@
     inside = lax.ppermute(inside, "py", inside_pairs)
     done = pl.pallas_call(
         sections_kernel,
-        out_shape=jax.ShapeDtypeStruct((8, 2, 8, LANES), jnp.float32),
-        in_specs=vmem(3),
+        out_shape=jax.ShapeDtypeStruct((128, LANES), jnp.float32),
+        in_specs=vmem(4),
         out_specs=vmem(1)[0],
         compiler_params=PARAMS,
         name="sections",
-    )(rows, inside, cross)
+    )(rows, inside, cross, tables)
     back = lax.all_to_all(done.reshape(16, 8, LANES), ("px", "lev"), 0, 0, tiled=True)
     return pl.pallas_call(
         remap_kernel,
@@ -251,6 +296,4 @@
         P(),
     )
     out_specs = P(None, "lev", "px", "py")
-    return jax.shard_map(
-        step, mesh=mesh, in_specs=in_specs, out_specs=out_specs, check_vma=False
-    )
+    return jax.shard_map(step, mesh=mesh, in_specs=in_specs, out_specs=out_specs, check_vma=False)

time: 55.4 us -> 54.3 us (0.980)
  local copies, waits for them, and re-layouts: 1.47 us -> 0.78 us
    broadcast_in_dim x3 -> x0, local copies, waits for them, and re-layouts: 0.71 us -> none  [step(): jnp.broadcast_to(part[None], whole)]
    pallas_call x1 -> x3, Pallas kernels: 1.54 us -> 1.18 us  [the longest x1 1.16 us: step(): pl.pallas_call(sections_kernel, out_shape=jax.ShapeDtypeStruct((128, LANE...]
where the time goes in v3:
time: 54.3 us; the launch traced here: 54 us
  blocking collectives  28.4 us (52%)
  starting transfers between devices  21.1 us (39%)
  Pallas kernels  2.04 us (4%)
  waiting for transfers between devices  1.58 us (3%)
  local copies, waits for them, and re-layouts  0.78 us (1%)
    ppermute x1, starting transfers between devices, step(): cross = lax.ppermute(cross, 'py', cross_pairs)  19.1 us
    all_to_all x1, blocking collectives, step(): rows = lax.all_to_all(packed, 'px', 0, 0, tiled=True).reshape(256, LANES)  16.5 us
    all_to_all x1, blocking collectives, step(): lax.all_to_all(done.reshape(16, 8, LANES), ('px', 'lev'), 0, 0, tiled=True)  12 us
    ppermute x1, starting transfers between devices, step(): inside = lax.ppermute(inside, 'py', inside_pairs)  1.92 us
    ppermute x1, waiting for transfers between devices, step(): cross = lax.ppermute(cross, 'py', cross_pairs)  1.57 us
    pallas_call x1, Pallas kernels, step(): pl.pallas_call(sections_kernel, out_shape=jax.ShapeDtypeStruct((128, LANE...  1.16 us
  transfers between devices with their start and end apart: 2, of which 1 were waited for; matrix products, arithmetic and copies ran while one was open for 0% of the time, Pallas kernels for 0%

profile of v3, /device:TPU:14, one launch (start us, length us, event | category | flops | bytes accessed | tf_op | source)
XLA Modules:
  0.0 54.0 jit_solution(4880722049907478500)
XLA Ops:
  0.0 0.0 copy-start.3
  0.0 0.0 copy-start.2
  0.0 0.0 copy-start.1
  0.0 0.0 copy-start
  0.0 0.7 %copy-done.3 = f32[1,8,128]{2,1,0:T(8,128)S(1)} copy-done((f32[1,8,128]{2,1,0:T(8,128)S(1)}, f32[1,8,128]{2,1,0:T(8,128)}, u32[]{:S(2)}) %copy-start.3) | copy-done | bytes 4120
  0.7 0.0 copy-done.2
  0.7 0.0 copy-done.1
  0.7 0.1 copy-done
  0.8 16.5 %all_to_all.10 = f32[8,4,8,128]{3,2,1,0:T(8,128)S(1)} all-to-all(f32[8,4,8,128]{3,2,1,0:T(8,128)S(1)} %pack.1), channel_id=1, replica_groups=mesh['px'=8,'py'=64,'lev'=2] {'px'}, dimensions={0} | all-to-all | bytes 262144 | tf_op jit(solution)/shard_map/all_to_all | solution.py:257
  17.3 0.1 edges.1
  17.4 1.9 %collective-permute-start = (f32[8,8,128]{2,1,0:T(8,128)S(1)}, f32[8,8,128]{2,1,0:T(8,128)S(1)}, u32[]{:S(2)}, u32[]{:S(2)}) collective-permute-start(f32[8,8,128]{2,1,0:T(8,128)S(1)} %get-tuple-element.7), channel_id=1, source_target_pairs={{0,2},{2,0},{4,6},{6,4},{8,10},{10,8},{12,14},{14,12},{16,18},{18,... | collective-permute-start | bytes 98312 | tf_op jit(solution)/shard_map/ppermute | solution.py:270
  19.4 19.1 %collective-permute-start.1 = (f32[8,8,128]{2,1,0:T(8,128)S(1)}, f32[8,8,128]{2,1,0:T(8,128)S(1)}, u32[]{:S(2)}, u32[]{:S(2)}) collective-permute-start(f32[8,8,128]{2,1,0:T(8,128)S(1)} %get-tuple-element.8), channel_id=1, source_target_pairs={{2,4},{4,2},{6,8},{8,6},{10,12},{12,10},{14,16},{16,14},{18,20},{2... | collective-permute-start | bytes 98312 | tf_op jit(solution)/shard_map/ppermute | solution.py:269
  38.5 0.0 collective-permute-done.in_ref
  38.5 1.6 %collective-permute-done.1.cross_ref = f32[8,8,128]{2,1,0:T(8,128)S(1)} collective-permute-done((f32[8,8,128]{2,1,0:T(8,128)S(1)}, f32[8,8,128]{2,1,0:T(8,128)S(1)}, u32[]{:S(2)}, u32[]{:S(2)}) %collective-permute-start.1) | collective-permute-done | bytes 32800 | tf_op jit(solution)/shard_map/ppermute | solution.py:269
  40.1 1.2 %sections.1 = f32[128,128]{1,0:T(8,128)S(1)} custom-call(f32[256,128]{1,0:T(8,128)S(1)} %bitcast.3, f32[8,8,128]{2,1,0:T(8,128)S(1)} %collective-permute-done.in_ref, f32[8,8,128]{2,1,0:T(8,128)S(1)} %collective-permute-done.1.cross_ref, f32[4,8,128]{2,1,0:T(8,128)S(1)} %tables.1.first_ref.table_ref), custom_call_target="tpu_custom_call" | custom-call | tf_op jit(solution)/shard_map/sections/pallas_call | solution.py:271
  41.3 0.0 copy-start.4
  41.3 12.0 %all_to_all.11.x_ref = f32[16,8,128]{2,1,0:T(8,128)S(1)} all-to-all(f32[16,8,128]{2,1,0:T(8,128)S(1)} %bitcast.4), channel_id=1, replica_groups=mesh['px'=8,'py'=64,'lev'=2] {'px','lev'}, dimensions={0} | all-to-all | bytes 131072 | tf_op jit(solution)/shard_map/all_to_all | solution.py:279
  53.3 0.0 copy-done.4
  53.3 0.7 %remap.1 = f32[2,4,8,128]{3,2,1,0:T(8,128)} custom-call(f32[2,2]{1,0:T(2,128)S(1)} %copy-done.4, f32[16,8,128]{2,1,0:T(8,128)S(1)} %all_to_all.11.x_ref), custom_call_target="tpu_custom_call" | custom-call | tf_op jit(solution)/shard_map/remap/pallas_call | solution.py:280
  (2 shorter events, 0.0 us)
Async XLA Ops:
  0.0 0.7 %copy-start.3 = (f32[1,8,128]{2,1,0:T(8,128)S(1)}, f32[1,8,128]{2,1,0:T(8,128)}, u32[]{:S(2)}) copy-start(f32[1,8,128]{2,1,0:T(8,128)} %y_ref.1) | copy-start | bytes 12292
  0.0 0.7 %copy-start.2 = (f32[1,8,128]{2,1,0:T(8,128)S(1)}, f32[1,8,128]{2,1,0:T(8,128)}, u32[]{:S(2)}) copy-start(f32[1,8,128]{2,1,0:T(8,128)} %x_ref.1) | copy-start | bytes 12292
  0.0 0.7 %copy-start.1 = (f32[1,8,128]{2,1,0:T(8,128)S(1)}, f32[1,8,128]{2,1,0:T(8,128)}, u32[]{:S(2)}) copy-start(f32[1,8,128]{2,1,0:T(8,128)} %m_ref.1) | copy-start | bytes 12292
  0.0 0.8 %copy-start = (f32[1,8,8,128]{3,2,1,0:T(8,128)S(1)}, f32[1,8,8,128]{3,2,1,0:T(8,128)}, u32[]{:S(2)}) copy-start(f32[1,8,8,128]{3,2,1,0:T(8,128)} %t_ref.1) | copy-start | bytes 98308
  17.4 21.1 %collective-permute-start = (f32[8,8,128]{2,1,0:T(8,128)S(1)}, f32[8,8,128]{2,1,0:T(8,128)S(1)}, u32[]{:S(2)}, u32[]{:S(2)}) collective-permute-start(f32[8,8,128]{2,1,0:T(8,128)S(1)} %get-tuple-element.7), channel_id=1, source_target_pairs={{0,2},{2,0},{4,6},{6,4},{8,10},{10,8},{12,14},{14,12},{16,18},{18,... | collective-permute-start | bytes 98312 | tf_op jit(solution)/shard_map/ppermute | solution.py:270
  19.4 20.7 %collective-permute-start.1 = (f32[8,8,128]{2,1,0:T(8,128)S(1)}, f32[8,8,128]{2,1,0:T(8,128)S(1)}, u32[]{:S(2)}, u32[]{:S(2)}) collective-permute-start(f32[8,8,128]{2,1,0:T(8,128)S(1)} %get-tuple-element.8), channel_id=1, source_target_pairs={{2,4},{4,2},{6,8},{8,6},{10,12},{12,10},{14,16},{16,14},{18,20},{2... | collective-permute-start | bytes 98312 | tf_op jit(solution)/shard_map/ppermute | solution.py:269
  41.3 12.0 %copy-start.4 = (f32[2,2]{1,0:T(2,128)S(1)}, f32[2,2]{1,0:T(2,128)}, u32[]{:S(2)}) copy-start(f32[2,2]{1,0:T(2,128)} %remap_ref.1) | copy-start | bytes 52

commit v4 on v3

v4 whole, which is shorter than its diff:
```python
import functools

import jax
import jax.numpy as jnp
import numpy as np
from jax import lax
from jax.experimental import pallas as pl
from jax.experimental.pallas import tpu as pltpu
from jax.sharding import PartitionSpec as P

GLL_NODES = 4
LANES = 128
PARAMS = pltpu.CompilerParams(vmem_limit_bytes=8 * 1024 * 1024)
SLOT = 32
WINDOW = 96
HALO = 24

sentinel = 1e30
step_size = 0.1
section_weights = ((0.0, 1.0), (0.75, 0.25), (1.0 / 3.0, 2.0 / 3.0))


def derivative_table():
    points = np.array([-1.0, -(5.0 ** (-0.5)), 5.0 ** (-0.5), 1.0])
    number = points.shape[0]
    barycentric = np.array(
        [
            1.0
            / np.prod([points[outer] - points[inner] for inner in range(number) if inner != outer])
            for outer in range(number)
        ]
    )
    table = np.zeros((number, number))
    for outer in range(number):
        for inner in range(number):
            if inner != outer:
                table[outer, inner] = (
                    barycentric[inner] / barycentric[outer] / (points[outer] - points[inner])
                )
    for outer in range(number):
        table[outer, outer] = -np.sum(table[outer])
    return table


def rot(x, k):
    k = k % LANES
    return pltpu.roll(x, k, 1) if k else x


def lane_index():
    return lax.broadcasted_iota(jnp.int32, (8, LANES), 1)


def node_index():
    return lane_index() % GLL_NODES


def table_kernel(out_ref):
    table = derivative_table() * step_size
    node = node_index()
    for m in range(4):
        c = jnp.full((8, LANES), table[0, m], jnp.float32)
        for i in range(1, 4):
            c = jnp.where(node == i, jnp.float32(table[i, i ^ m]), c)
        out_ref[m] = c


def pack_kernel(first_ref, t_ref, m_ref, x_ref, y_ref, out_ref):
    window = lane_index() < WINDOW
    for half in range(2):
        shift = -SLOT * half
        piece = [rot(y_ref[0], WINDOW - SLOT * u + shift) for u in range(3)]
        mass = jnp.where(window, rot(m_ref[0], shift), piece[2])
        wind = rot(x_ref[0], shift)
        for q in range(4):
            for u in range(2):
                t = rot(t_ref[0, 2 * q + u], shift)
                out_ref[2 * q + half, u] = jnp.where(window, t, piece[u])
            out_ref[2 * q + half, 2] = mass
            out_ref[2 * q + half, 3] = wind


def gathered(r_ref, u, r):
    return r_ref[pl.ds(u * 8 + r, 8, stride=32), :]


def moved_lanes(x, left, if_left, if_right):
    return pltpu.roll(x, jnp.where(left, if_left % LANES, if_right % LANES), 1)


def edge_kernel(r_ref, out_ref):
    slot = lane_index() // HALO
    left = lax.axis_index("px") % 2 == 0
    for r in range(8):
        unit = [gathered(r_ref, u, r) for u in range(4)]
        edge = moved_lanes(jnp.where(left, unit[0], unit[2]), left, 0, -8)
        for a in range(4):
            piece = moved_lanes(unit[a], left, HALO * a, HALO * a + HALO - WINDOW)
            edge = jnp.where(slot == a, piece, edge)
        out_ref[r] = edge


def sections_kernel(r_ref, halo_ref, table_ref, out_ref):
    lane = lane_index()
    node = node_index()
    py = lax.axis_index("py")
    left = lax.axis_index("px") % 2 == 0
    has_halo = (left & (py > 0)) | (~left & (py < lax.axis_size("py") - 1))
    exists = (lane < WINDOW) | has_halo
    inner_end = jnp.where(left, LANES, WINDOW + HALO)
    in_halo = (lane >= inner_end - HALO) & (lane < inner_end)
    rim_node = (node == 0) | (node == 3)
    partner = jnp.where(node == 0, lane - 1, jnp.where(node == 3, lane + 1, lane))
    partner = (partner + LANES) % LANES
    table = derivative_table() * step_size
    rows = range(8)

    def permuted(x, index):
        return jnp.take_along_axis(x, index, axis=1, mode="promise_in_bounds")

    def completed(a, fill):
        result = []
        for r in rows:
            if a < 4:
                x = gathered(r_ref, a, r)
            else:
                unit = [gathered(r_ref, u, r) for u in range(3)]
                x = jnp.where(lane < 2 * SLOT, rot(unit[1], 2 * SLOT), rot(unit[2], 3 * SLOT))
                x = jnp.where(lane < SLOT, rot(unit[0], SLOT), x)
            halo = moved_lanes(halo_ref[r], left, LANES - HALO - HALO * a, WINDOW - HALO * a)
            halo = jnp.where(in_halo, halo, jnp.float32(fill))
            result.append(jnp.where(lane < WINDOW, x, halo))
        return result

    def up(x):
        return pltpu.roll(x, 1, 0)

    def down(x):
        return pltpu.roll(x, 7, 0)

    def shared(f):
        f = list(f)
        first, last = f[0], f[7]
        f[0] = first + up(last)
        f[7] = last + down(first)
        f[3] = f[4] = f[3] + f[4]
        return [x + jnp.where(rim_node, permuted(x, partner), 0.0) for x in f]

    def extreme(f, op, missing):
        halves = []
        for e in range(2):
            x = op(op(f[4 * e], f[4 * e + 1]), op(f[4 * e + 2], f[4 * e + 3]))
            x = op(x, permuted(x, lane ^ 1))
            x = op(x, permuted(x, lane ^ 2))
            x = jnp.where(exists, x, missing)
            halves.append(op(op(x, rot(x, 4)), rot(x, -4)))
        zero, one = halves
        both = op(zero, one)
        return op(both, up(one)), op(both, down(zero))

    def slopes_x(f):
        outer, inner = f[0] - f[3], f[1] - f[2]
        even_part = (f[0] + f[3]) - (f[1] + f[2])
        result = [None] * 4
        for i in range(2):
            p = jnp.float32((table[i, 0] - table[i, 3]) / 2) * outer
            p = p + jnp.float32((table[i, 1] - table[i, 2]) / 2) * inner
            q = jnp.float32((table[i, 0] + table[i, 3]) / 2) * even_part
            result[i], result[3 - i] = p + q, p - q
        return result

    mass = completed(2, 1.0)
    wind_x = completed(3, 0.0)
    wind_y = completed(4, 0.0)
    coefficient = [table_ref[m] for m in range(4)]
    inverse = [jnp.where(exists, 1.0 / jnp.where(exists, m, 1.0), 0.0) for m in shared(mass)]
    finished = []
    for tracer in range(2):
        start = completed(tracer, 0.0)
        field = start
        for share_start, share_new in section_weights:
            lower = extreme(field, jnp.minimum, sentinel)
            upper = extreme(field, jnp.maximum, -sentinel)
            weighted = [None] * 8
            for e in range(2):
                along_x = slopes_x([wind_x[4 * e + i] * field[4 * e + i] for i in range(4)])
                for i in range(4):
                    r = 4 * e + i
                    flux_y = wind_y[r] * field[r]
                    slope = along_x[i] + coefficient[0] * flux_y
                    for m in range(1, 4):
                        slope = slope + coefficient[m] * permuted(flux_y, lane ^ m)
                    limited = jnp.minimum(jnp.maximum(field[r] - slope, lower[e]), upper[e])
                    weighted[r] = mass[r] * limited
            summed = shared(weighted)
            fresh = [None] * 8
            for r in rows:
                value = summed[r] * inverse[r]
                if share_new != 1.0:
                    value = jnp.float32(share_new) * value
                if share_start:
                    value = jnp.float32(share_start) * start[r] + value
                fresh[r] = value
            field = fresh
        finished.append(field)
    for r in rows:
        low = moved_lanes(finished[0][r], left, 0, -SLOT)
        high = moved_lanes(finished[1][r], left, 2 * SLOT, SLOT)
        both = jnp.where(lane < 2 * SLOT, low, high)
        for m in range(2):
            out_ref[pl.ds(m * 8 + r, 8, stride=16), :] = both


def remap_kernel(remap_ref, x_ref, out_ref):
    base = lax.axis_index("lev") * 8
    low = lane_index() < LANES // 2
    weight = [[remap_ref[a : a + 1, b : b + 1] for b in range(2)] for a in range(2)]
    for q in range(2):
        first, second = [], []
        for level in range(2):
            left = x_ref[base + 4 * q + level]
            right = x_ref[base + 4 * q + 2 + level]
            first.append(jnp.where(low, left, rot(right, LANES // 2)))
            second.append(jnp.where(low, rot(left, LANES // 2), right))
        for a in range(2):
            out_ref[a, 2 * q] = weight[a][0] * first[0] + weight[a][1] * first[1]
            out_ref[a, 2 * q + 1] = weight[a][0] * second[0] + weight[a][1] * second[1]


def vmem(count):
    return [pl.BlockSpec(memory_space=pltpu.VMEM)] * count


def shards(tracer, node_mass, wind_x, wind_y, remap):
    count = lax.axis_size("py")
    tables = pl.pallas_call(
        table_kernel,
        out_shape=jax.ShapeDtypeStruct((4, 8, LANES), jnp.float32),
        out_specs=vmem(1)[0],
        compiler_params=PARAMS,
        cost_estimate=pl.CostEstimate(flops=10**10, bytes_accessed=10**7, transcendentals=0),
        name="tables",
    )()
    packed = pl.pallas_call(
        pack_kernel,
        out_shape=jax.ShapeDtypeStruct((8, 4, 8, LANES), jnp.float32),
        in_specs=vmem(5),
        out_specs=vmem(1)[0],
        compiler_params=PARAMS,
        name="pack",
    )(tables, tracer, node_mass, wind_x, wind_y)
    rows = lax.all_to_all(packed, "px", 0, 0, tiled=True).reshape(256, LANES)
    edge = pl.pallas_call(
        edge_kernel,
        out_shape=jax.ShapeDtypeStruct((8, 8, LANES), jnp.float32),
        in_specs=vmem(1),
        out_specs=vmem(1)[0],
        compiler_params=PARAMS,
        name="edge",
    )(rows)
    pairs = []
    for q in range(0, lax.axis_size("px"), 2):
        for py in range(1, count):
            a, b = q * count + py, (q + 1) * count + py - 1
            pairs += [(a, b), (b, a)]
    halo = lax.ppermute(edge, ("px", "py"), pairs)
    done = pl.pallas_call(
        sections_kernel,
        out_shape=jax.ShapeDtypeStruct((128, LANES), jnp.float32),
        in_specs=vmem(3),
        out_specs=vmem(1)[0],
        compiler_params=PARAMS,
        name="sections",
    )(rows, halo, tables)
    back = lax.all_to_all(done.reshape(16, 8, LANES), ("px", "lev"), 0, 0, tiled=True)
    return pl.pallas_call(
        remap_kernel,
        out_shape=jax.ShapeDtypeStruct((2, 4, 8, LANES), jnp.float32),
        in_specs=vmem(2),
        out_specs=vmem(1)[0],
        compiler_params=PARAMS,
        name="remap",
    )(remap, back)


def solution(mesh):
    in_specs = (
        P("lev", None, "px", "py"),
        P("lev", "px", "py"),
        P("lev", "px", "py"),
        P("lev", "px", "py"),
        P(),
    )
    out_specs = P(None, "lev", "px", "py")
    return jax.shard_map(shards, mesh=mesh, in_specs=in_specs, out_specs=out_specs, check_vma=False)
```

time: 54.3 us -> 50.3 us (0.926)
  starting transfers between devices: 21.1 us -> 17 us
    ppermute x2 -> x1, starting transfers between devices: 21.1 us -> 17 us  [shards(): halo = lax.ppermute(edge, ('px', 'py'), pairs)]
    ppermute x2 -> x1, waiting for transfers between devices: 1.58 us -> 1.58 us  [shards(): halo = lax.ppermute(edge, ('px', 'py'), pairs)]
  transfers between devices with their start and end apart: 2 -> 1, of which waited for: 1 -> 1; matrix products, arithmetic and copies ran while one was open for 0% -> 0% of each run, Pallas kernels for 0% -> 0%
where the time goes in v4:
time: 50.3 us; the launch traced here: 50.1 us
  blocking collectives  28.4 us (56%)
  starting transfers between devices  17 us (34%)
  Pallas kernels  2.17 us (4%)
  waiting for transfers between devices  1.58 us (3%)
  local copies, waits for them, and re-layouts  0.78 us (2%)
    ppermute x1, starting transfers between devices, shards(): halo = lax.ppermute(edge, ('px', 'py'), pairs)  17 us
    all_to_all x1, blocking collectives, shards(): rows = lax.all_to_all(packed, 'px', 0, 0, tiled=True).reshape(256, LANES)  16.5 us
    all_to_all x1, blocking collectives, shards(): lax.all_to_all(done.reshape(16, 8, LANES), ('px', 'lev'), 0, 0, tiled=True)  12 us
    ppermute x1, waiting for transfers between devices, shards(): halo = lax.ppermute(edge, ('px', 'py'), pairs)  1.58 us
    pallas_call x1, Pallas kernels, shards(): pl.pallas_call(sections_kernel, out_shape=jax.ShapeDtypeStruct((128, LANE...  1.22 us
  transfers between devices with their start and end apart: 1, of which 1 were waited for; matrix products, arithmetic and copies ran while one was open for 0% of the time, Pallas kernels for 0%

profile of v4, /device:TPU:14, one launch (start us, length us, event | category | flops | bytes accessed | tf_op | source)
XLA Modules:
  0.0 50.1 jit_solution(8278653108916454393)
XLA Ops:
  0.0 0.0 copy-start.3
  0.0 0.0 copy-start.2
  0.0 0.0 copy-start.1
  0.0 0.0 copy-start
  0.0 0.7 %copy-done.3 = f32[1,8,128]{2,1,0:T(8,128)S(1)} copy-done((f32[1,8,128]{2,1,0:T(8,128)S(1)}, f32[1,8,128]{2,1,0:T(8,128)}, u32[]{:S(2)}) %copy-start.3) | copy-done | bytes 4120
  0.7 0.0 copy-done.2
  0.7 0.0 copy-done.1
  0.7 0.1 copy-done
  0.8 0.1 pack.1
  0.9 16.5 %all_to_all.10 = f32[8,4,8,128]{3,2,1,0:T(8,128)S(1)} all-to-all(f32[8,4,8,128]{3,2,1,0:T(8,128)S(1)} %pack.1), channel_id=1, replica_groups=mesh['px'=8,'py'=64,'lev'=2] {'px'}, dimensions={0} | all-to-all | bytes 262144 | tf_op jit(solution)/shard_map/all_to_all | solution.py:252
  17.4 0.1 edge.1
  17.5 17.0 %collective-permute-start = (f32[8,8,128]{2,1,0:T(8,128)S(1)}, f32[8,8,128]{2,1,0:T(8,128)S(1)}, u32[]{:S(2)}, u32[]{:S(2)}) collective-permute-start(f32[8,8,128]{2,1,0:T(8,128)S(1)} %edge.1), channel_id=1, source_target_pairs={{2,128},{128,2},{4,130},{130,4},{6,132},{132,6},{8,134},{134,8},{1... | collective-permute-start | bytes 98312 | tf_op jit(solution)/shard_map/ppermute | solution.py:266
  34.5 1.6 %collective-permute-done.halo_ref = f32[8,8,128]{2,1,0:T(8,128)S(1)} collective-permute-done((f32[8,8,128]{2,1,0:T(8,128)S(1)}, f32[8,8,128]{2,1,0:T(8,128)S(1)}, u32[]{:S(2)}, u32[]{:S(2)}) %collective-permute-start) | collective-permute-done | bytes 32800 | tf_op jit(solution)/shard_map/ppermute | solution.py:266
  36.1 1.2 %sections.1 = f32[128,128]{1,0:T(8,128)S(1)} custom-call(f32[256,128]{1,0:T(8,128)S(1)} %bitcast.3, f32[8,8,128]{2,1,0:T(8,128)S(1)} %collective-permute-done.halo_ref, f32[4,8,128]{2,1,0:T(8,128)S(1)} %tables.1.first_ref.table_ref), custom_call_target="tpu_custom_call" | custom-call | tf_op jit(solution)/shard_map/sections/pallas_call | solution.py:267
  37.4 0.0 copy-start.4
  37.4 12.0 %all_to_all.11.x_ref = f32[16,8,128]{2,1,0:T(8,128)S(1)} all-to-all(f32[16,8,128]{2,1,0:T(8,128)S(1)} %bitcast.4), channel_id=1, replica_groups=mesh['px'=8,'py'=64,'lev'=2] {'px','lev'}, dimensions={0} | all-to-all | bytes 131072 | tf_op jit(solution)/shard_map/all_to_all | solution.py:275
  49.3 0.0 copy-done.4
  49.3 0.7 %remap.1 = f32[2,4,8,128]{3,2,1,0:T(8,128)} custom-call(f32[2,2]{1,0:T(2,128)S(1)} %copy-done.4, f32[16,8,128]{2,1,0:T(8,128)S(1)} %all_to_all.11.x_ref), custom_call_target="tpu_custom_call" | custom-call | tf_op jit(solution)/shard_map/remap/pallas_call | solution.py:276
  (1 shorter events, 0.0 us)
Async XLA Ops:
  0.0 0.7 %copy-start.3 = (f32[1,8,128]{2,1,0:T(8,128)S(1)}, f32[1,8,128]{2,1,0:T(8,128)}, u32[]{:S(2)}) copy-start(f32[1,8,128]{2,1,0:T(8,128)} %y_ref.1) | copy-start | bytes 12292
  0.0 0.7 %copy-start.2 = (f32[1,8,128]{2,1,0:T(8,128)S(1)}, f32[1,8,128]{2,1,0:T(8,128)}, u32[]{:S(2)}) copy-start(f32[1,8,128]{2,1,0:T(8,128)} %x_ref.1) | copy-start | bytes 12292
  0.0 0.7 %copy-start.1 = (f32[1,8,128]{2,1,0:T(8,128)S(1)}, f32[1,8,128]{2,1,0:T(8,128)}, u32[]{:S(2)}) copy-start(f32[1,8,128]{2,1,0:T(8,128)} %m_ref.1) | copy-start | bytes 12292
  0.0 0.8 %copy-start = (f32[1,8,8,128]{3,2,1,0:T(8,128)S(1)}, f32[1,8,8,128]{3,2,1,0:T(8,128)}, u32[]{:S(2)}) copy-start(f32[1,8,8,128]{3,2,1,0:T(8,128)} %t_ref.1) | copy-start | bytes 98308
  17.5 18.6 %collective-permute-start = (f32[8,8,128]{2,1,0:T(8,128)S(1)}, f32[8,8,128]{2,1,0:T(8,128)S(1)}, u32[]{:S(2)}, u32[]{:S(2)}) collective-permute-start(f32[8,8,128]{2,1,0:T(8,128)S(1)} %edge.1), channel_id=1, source_target_pairs={{2,128},{128,2},{4,130},{130,4},{6,132},{132,6},{8,134},{134,8},{1... | collective-permute-start | bytes 98312 | tf_op jit(solution)/shard_map/ppermute | solution.py:266
  37.4 12.0 %copy-start.4 = (f32[2,2]{1,0:T(2,128)S(1)}, f32[2,2]{1,0:T(2,128)}, u32[]{:S(2)}) copy-start(f32[2,2]{1,0:T(2,128)} %remap_ref.1) | copy-start | bytes 52

commit v5 on v4

--- a/solution.py
+++ b/solution.py
@@ -66,31 +66,37 @@
 
 
 def pack_kernel(first_ref, t_ref, m_ref, x_ref, y_ref, out_ref):
+    odd = lax.axis_index("py") % 2
     window = lane_index() < WINDOW
     for half in range(2):
         shift = -SLOT * half
         piece = [rot(y_ref[0], WINDOW - SLOT * u + shift) for u in range(3)]
         mass = jnp.where(window, rot(m_ref[0], shift), piece[2])
         wind = rot(x_ref[0], shift)
+        place = jnp.where(odd == 1, 1 - half, half)
         for q in range(4):
             for u in range(2):
                 t = rot(t_ref[0, 2 * q + u], shift)
-                out_ref[2 * q + half, u] = jnp.where(window, t, piece[u])
-            out_ref[2 * q + half, 2] = mass
-            out_ref[2 * q + half, 3] = wind
+                out_ref[2 * q + place, u] = jnp.where(window, t, piece[u])
+            out_ref[2 * q + place, 2] = mass
+            out_ref[2 * q + place, 3] = wind
 
 
 def gathered(r_ref, u, r):
     return r_ref[pl.ds(u * 8 + r, 8, stride=32), :]
 
 
+def works_left():
+    return (lax.axis_index("px") + lax.axis_index("py")) % 2 == 0
+
+
 def moved_lanes(x, left, if_left, if_right):
     return pltpu.roll(x, jnp.where(left, if_left % LANES, if_right % LANES), 1)
 
 
 def edge_kernel(r_ref, out_ref):
     slot = lane_index() // HALO
-    left = lax.axis_index("px") % 2 == 0
+    left = works_left()
     for r in range(8):
         unit = [gathered(r_ref, u, r) for u in range(4)]
         edge = moved_lanes(jnp.where(left, unit[0], unit[2]), left, 0, -8)
@@ -100,11 +106,22 @@
         out_ref[r] = edge
 
 
-def sections_kernel(r_ref, halo_ref, table_ref, out_ref):
+def collect_kernel(r_ref, out_ref):
+    lane = lane_index()
+    for r in range(8):
+        unit = [gathered(r_ref, u, r) for u in range(4)]
+        last = jnp.where(lane < 2 * SLOT, rot(unit[1], 2 * SLOT), rot(unit[2], 3 * SLOT))
+        last = jnp.where(lane < SLOT, rot(unit[0], SLOT), last)
+        for a in range(4):
+            out_ref[a, r] = unit[a]
+        out_ref[4, r] = last
+
+
+def sections_kernel(own_ref, halo_ref, table_ref, out_ref):
     lane = lane_index()
     node = node_index()
     py = lax.axis_index("py")
-    left = lax.axis_index("px") % 2 == 0
+    left = works_left()
     has_halo = (left & (py > 0)) | (~left & (py < lax.axis_size("py") - 1))
     exists = (lane < WINDOW) | has_halo
     inner_end = jnp.where(left, LANES, WINDOW + HALO)
@@ -121,15 +138,9 @@
     def completed(a, fill):
         result = []
         for r in rows:
-            if a < 4:
-                x = gathered(r_ref, a, r)
-            else:
-                unit = [gathered(r_ref, u, r) for u in range(3)]
-                x = jnp.where(lane < 2 * SLOT, rot(unit[1], 2 * SLOT), rot(unit[2], 3 * SLOT))
-                x = jnp.where(lane < SLOT, rot(unit[0], SLOT), x)
             halo = moved_lanes(halo_ref[r], left, LANES - HALO - HALO * a, WINDOW - HALO * a)
             halo = jnp.where(in_halo, halo, jnp.float32(fill))
-            result.append(jnp.where(lane < WINDOW, x, halo))
+            result.append(jnp.where(lane < WINDOW, own_ref[a, r], halo))
         return result
 
     def up(x):
@@ -208,18 +219,19 @@
         high = moved_lanes(finished[1][r], left, 2 * SLOT, SLOT)
         both = jnp.where(lane < 2 * SLOT, low, high)
         for m in range(2):
-            out_ref[pl.ds(m * 8 + r, 8, stride=16), :] = both
+            out_ref[pl.ds(m * 64 + r, 8, stride=8), :] = both
 
 
 def remap_kernel(remap_ref, x_ref, out_ref):
-    base = lax.axis_index("lev") * 8
+    base = lax.axis_index("lev") * 4
+    odd = lax.axis_index("py") % 2
     low = lane_index() < LANES // 2
     weight = [[remap_ref[a : a + 1, b : b + 1] for b in range(2)] for a in range(2)]
     for q in range(2):
         first, second = [], []
         for level in range(2):
-            left = x_ref[base + 4 * q + level]
-            right = x_ref[base + 4 * q + 2 + level]
+            left = x_ref[base + 2 * q + odd + 8 * level]
+            right = x_ref[base + 2 * q + 1 - odd + 8 * level]
             first.append(jnp.where(low, left, rot(right, LANES // 2)))
             second.append(jnp.where(low, rot(left, LANES // 2), right))
         for a in range(2):
@@ -259,11 +271,20 @@
         name="edge",
     )(rows)
     pairs = []
-    for q in range(0, lax.axis_size("px"), 2):
-        for py in range(1, count):
-            a, b = q * count + py, (q + 1) * count + py - 1
-            pairs += [(a, b), (b, a)]
+    for px in range(lax.axis_size("px")):
+        for py in range(2 - px % 2, count, 2):
+            a = px * count + py
+            pairs += [(a, a - 1), (a - 1, a)]
     halo = lax.ppermute(edge, ("px", "py"), pairs)
+    own = pl.pallas_call(
+        collect_kernel,
+        out_shape=jax.ShapeDtypeStruct((5, 8, 8, LANES), jnp.float32),
+        in_specs=vmem(1),
+        out_specs=vmem(1)[0],
+        compiler_params=PARAMS,
+        cost_estimate=pl.CostEstimate(flops=10**5, bytes_accessed=300000, transcendentals=0),
+        name="collect",
+    )(rows)
     done = pl.pallas_call(
         sections_kernel,
         out_shape=jax.ShapeDtypeStruct((128, LANES), jnp.float32),
@@ -271,8 +292,8 @@
         out_specs=vmem(1)[0],
         compiler_params=PARAMS,
         name="sections",
-    )(rows, halo, tables)
-    back = lax.all_to_all(done.reshape(16, 8, LANES), ("px", "lev"), 0, 0, tiled=True)
+    )(own, halo, tables)
+    back = lax.all_to_all(done.reshape(16, 8, LANES), ("lev", "px"), 0, 0, tiled=True)
     return pl.pallas_call(
         remap_kernel,
         out_shape=jax.ShapeDtypeStruct((2, 4, 8, LANES), jnp.float32),

time: 50.3 us -> 49.6 us (0.986)
    all_to_all x1, blocking collectives: 12 us -> 11.4 us  [shards(): lax.all_to_all(done.reshape(16, 8, LANES), ('lev', 'px'), 0, 0, tiled=True)]
where the time goes in v5:
time: 49.6 us; the launch traced here: 49.3 us
  blocking collectives  27.9 us (56%)
  starting transfers between devices  16.9 us (34%)
  Pallas kernels  2.27 us (5%)
  waiting for transfers between devices  1.45 us (3%)
  local copies, waits for them, and re-layouts  0.78 us (2%)
    ppermute x1, starting transfers between devices, shards(): halo = lax.ppermute(edge, ('px', 'py'), pairs)  16.9 us
    all_to_all x1, blocking collectives, shards(): rows = lax.all_to_all(packed, 'px', 0, 0, tiled=True).reshape(256, LANES)  16.5 us
    all_to_all x1, blocking collectives, shards(): lax.all_to_all(done.reshape(16, 8, LANES), ('lev', 'px'), 0, 0, tiled=True)  11.4 us
    ppermute x1, waiting for transfers between devices, shards(): halo = lax.ppermute(edge, ('px', 'py'), pairs)  1.45 us
    pallas_call x1, Pallas kernels, shards(): pl.pallas_call(sections_kernel, out_shape=jax.ShapeDtypeStruct((128, LANE...  1.2 us
  transfers between devices with their start and end apart: 1, of which 1 were waited for; matrix products, arithmetic and copies ran while one was open for 0% of the time, Pallas kernels for 0%

profile of v5, /device:TPU:14, one launch (start us, length us, event | category | flops | bytes accessed | tf_op | source)
XLA Modules:
  0.0 49.3 jit_solution(7210024717856839476)
XLA Ops:
  0.0 0.0 copy-start.3
  0.0 0.0 copy-start.2
  0.0 0.0 copy-start.1
  0.0 0.0 copy-start
  0.0 0.7 %copy-done.3 = f32[1,8,128]{2,1,0:T(8,128)S(1)} copy-done((f32[1,8,128]{2,1,0:T(8,128)S(1)}, f32[1,8,128]{2,1,0:T(8,128)}, u32[]{:S(2)}) %copy-start.3) | copy-done | bytes 4120
  0.7 0.0 copy-done.2
  0.7 0.0 copy-done.1
  0.7 0.1 copy-done
  0.8 0.1 pack.1
  0.9 16.5 %all_to_all.10 = f32[8,4,8,128]{3,2,1,0:T(8,128)S(1)} all-to-all(f32[8,4,8,128]{3,2,1,0:T(8,128)S(1)} %pack.1), channel_id=1, replica_groups=mesh['px'=8,'py'=64,'lev'=2] {'px'}, dimensions={0} | all-to-all | bytes 262144 | tf_op jit(solution)/shard_map/all_to_all | solution.py:264
  17.4 0.1 edge.1
  17.5 16.9 %collective-permute-start = (f32[8,8,128]{2,1,0:T(8,128)S(1)}, f32[8,8,128]{2,1,0:T(8,128)S(1)}, u32[]{:S(2)}, u32[]{:S(2)}) collective-permute-start(f32[8,8,128]{2,1,0:T(8,128)S(1)} %edge.1), channel_id=1, source_target_pairs={{4,2},{2,4},{8,6},{6,8},{12,10},{10,12},{16,14},{14,16},{20,18},{1... | collective-permute-start | bytes 98312 | tf_op jit(solution)/shard_map/ppermute | solution.py:278
  34.4 0.1 collect.1.own_ref
  34.5 1.5 %collective-permute-done.halo_ref = f32[8,8,128]{2,1,0:T(8,128)S(1)} collective-permute-done((f32[8,8,128]{2,1,0:T(8,128)S(1)}, f32[8,8,128]{2,1,0:T(8,128)S(1)}, u32[]{:S(2)}, u32[]{:S(2)}) %collective-permute-start) | collective-permute-done | bytes 32800 | tf_op jit(solution)/shard_map/ppermute | solution.py:278
  36.0 1.2 %sections.1 = f32[128,128]{1,0:T(8,128)S(1)} custom-call(f32[5,8,8,128]{3,2,1,0:T(8,128)S(1)} %collect.1.own_ref, f32[8,8,128]{2,1,0:T(8,128)S(1)} %collective-permute-done.halo_ref, f32[4,8,128]{2,1,0:T(8,128)S(1)} %tables.1.first_ref.table_ref), custom_call_target="tpu_custom_call" | custom-call | tf_op jit(solution)/shard_map/sections/pallas_call | solution.py:288
  37.2 0.0 copy-start.4
  37.2 11.4 %all_to_all.11.x_ref = f32[16,8,128]{2,1,0:T(8,128)S(1)} all-to-all(f32[16,8,128]{2,1,0:T(8,128)S(1)} %bitcast.4), channel_id=1, replica_groups=mesh['px'=8,'py'=64,'lev'=2] {'lev','px'}, dimensions={0} | all-to-all | bytes 131072 | tf_op jit(solution)/shard_map/all_to_all | solution.py:296
  48.6 0.0 copy-done.4
  48.6 0.7 %remap.1 = f32[2,4,8,128]{3,2,1,0:T(8,128)} custom-call(f32[2,2]{1,0:T(2,128)S(1)} %copy-done.4, f32[16,8,128]{2,1,0:T(8,128)S(1)} %all_to_all.11.x_ref), custom_call_target="tpu_custom_call" | custom-call | tf_op jit(solution)/shard_map/remap/pallas_call | solution.py:297
  (1 shorter events, 0.0 us)
Async XLA Ops:
  0.0 0.7 %copy-start.3 = (f32[1,8,128]{2,1,0:T(8,128)S(1)}, f32[1,8,128]{2,1,0:T(8,128)}, u32[]{:S(2)}) copy-start(f32[1,8,128]{2,1,0:T(8,128)} %y_ref.1) | copy-start | bytes 12292
  0.0 0.7 %copy-start.2 = (f32[1,8,128]{2,1,0:T(8,128)S(1)}, f32[1,8,128]{2,1,0:T(8,128)}, u32[]{:S(2)}) copy-start(f32[1,8,128]{2,1,0:T(8,128)} %x_ref.1) | copy-start | bytes 12292
  0.0 0.7 %copy-start.1 = (f32[1,8,128]{2,1,0:T(8,128)S(1)}, f32[1,8,128]{2,1,0:T(8,128)}, u32[]{:S(2)}) copy-start(f32[1,8,128]{2,1,0:T(8,128)} %m_ref.1) | copy-start | bytes 12292
  0.0 0.8 %copy-start = (f32[1,8,8,128]{3,2,1,0:T(8,128)S(1)}, f32[1,8,8,128]{3,2,1,0:T(8,128)}, u32[]{:S(2)}) copy-start(f32[1,8,8,128]{3,2,1,0:T(8,128)} %t_ref.1) | copy-start | bytes 98308
  17.5 18.5 %collective-permute-start = (f32[8,8,128]{2,1,0:T(8,128)S(1)}, f32[8,8,128]{2,1,0:T(8,128)S(1)}, u32[]{:S(2)}, u32[]{:S(2)}) collective-permute-start(f32[8,8,128]{2,1,0:T(8,128)S(1)} %edge.1), channel_id=1, source_target_pairs={{4,2},{2,4},{8,6},{6,8},{12,10},{10,12},{16,14},{14,16},{20,18},{1... | collective-permute-start | bytes 98312 | tf_op jit(solution)/shard_map/ppermute | solution.py:278
  37.2 11.4 %copy-start.4 = (f32[2,2]{1,0:T(2,128)S(1)}, f32[2,2]{1,0:T(2,128)}, u32[]{:S(2)}) copy-start(f32[2,2]{1,0:T(2,128)} %remap_ref.1) | copy-start | bytes 52

commit v6 on v5

--- a/solution.py
+++ b/solution.py
@@ -57,12 +57,17 @@
 
 def table_kernel(out_ref):
     table = derivative_table() * step_size
-    node = node_index()
-    for m in range(4):
-        c = jnp.full((8, LANES), table[0, m], jnp.float32)
-        for i in range(1, 4):
-            c = jnp.where(node == i, jnp.float32(table[i, i ^ m]), c)
-        out_ref[m] = c
+    source = lax.broadcasted_iota(jnp.int32, (LANES, LANES), 0)
+    target = lax.broadcasted_iota(jnp.int32, (LANES, LANES), 1)
+    place = (target % GLL_NODES) * GLL_NODES + source % GLL_NODES
+    c = jnp.zeros((LANES, LANES), jnp.float32)
+    for i in range(GLL_NODES):
+        for j in range(GLL_NODES):
+            c = jnp.where(place == i * GLL_NODES + j, jnp.float32(table[i, j]), c)
+    c = jnp.where(source // GLL_NODES == target // GLL_NODES, c, 0.0)
+    high = c.astype(jnp.bfloat16)
+    out_ref[0] = high
+    out_ref[1] = (c - high.astype(jnp.float32)).astype(jnp.bfloat16)
 
 
 def pack_kernel(first_ref, t_ref, m_ref, x_ref, y_ref, out_ref):
@@ -183,37 +188,42 @@
     mass = completed(2, 1.0)
     wind_x = completed(3, 0.0)
     wind_y = completed(4, 0.0)
-    coefficient = [table_ref[m] for m in range(4)]
     inverse = [jnp.where(exists, 1.0 / jnp.where(exists, m, 1.0), 0.0) for m in shared(mass)]
-    finished = []
-    for tracer in range(2):
-        start = completed(tracer, 0.0)
-        field = start
-        for share_start, share_new in section_weights:
-            lower = extreme(field, jnp.minimum, sentinel)
-            upper = extreme(field, jnp.maximum, -sentinel)
-            weighted = [None] * 8
-            for e in range(2):
+    starts = [completed(tracer, 0.0) for tracer in range(2)]
+    fields = list(starts)
+    for share_start, share_new in section_weights:
+        flux = jnp.concatenate([wind_y[r] * f[r] for f in fields for r in rows], axis=0)
+        high = flux.astype(jnp.bfloat16)
+        low = (flux - high.astype(jnp.float32)).astype(jnp.bfloat16)
+        both = jnp.concatenate([high, low], axis=0)
+        product = jnp.dot(both, table_ref[0], preferred_element_type=jnp.float32)
+        small = jnp.dot(high, table_ref[1], preferred_element_type=jnp.float32)
+        along_y = (product[128:] + small) + product[:128]
+        lowers = [extreme(f, jnp.minimum, sentinel) for f in fields]
+        uppers = [extreme(f, jnp.maximum, -sentinel) for f in fields]
+        weighted = [[None] * 8, [None] * 8]
+        for e in range(2):
+            for t in range(2):
+                field = fields[t]
                 along_x = slopes_x([wind_x[4 * e + i] * field[4 * e + i] for i in range(4)])
                 for i in range(4):
                     r = 4 * e + i
-                    flux_y = wind_y[r] * field[r]
-                    slope = along_x[i] + coefficient[0] * flux_y
-                    for m in range(1, 4):
-                        slope = slope + coefficient[m] * permuted(flux_y, lane ^ m)
-                    limited = jnp.minimum(jnp.maximum(field[r] - slope, lower[e]), upper[e])
-                    weighted[r] = mass[r] * limited
-            summed = shared(weighted)
-            fresh = [None] * 8
-            for r in rows:
-                value = summed[r] * inverse[r]
+                    at = 64 * t + 8 * r
+                    moved = field[r] - (along_x[i] + along_y[at : at + 8])
+                    limited = jnp.minimum(jnp.maximum(moved, lowers[t][e]), uppers[t][e])
+                    weighted[t][r] = mass[r] * limited
+        summed = [shared(w) for w in weighted]
+        fresh = [[None] * 8, [None] * 8]
+        for r in rows:
+            for t in range(2):
+                value = summed[t][r] * inverse[r]
                 if share_new != 1.0:
                     value = jnp.float32(share_new) * value
                 if share_start:
-                    value = jnp.float32(share_start) * start[r] + value
-                fresh[r] = value
-            field = fresh
-        finished.append(field)
+                    value = jnp.float32(share_start) * starts[t][r] + value
+                fresh[t][r] = value
+        fields = fresh
+    finished = fields
     for r in rows:
         low = moved_lanes(finished[0][r], left, 0, -SLOT)
         high = moved_lanes(finished[1][r], left, 2 * SLOT, SLOT)
@@ -247,7 +257,7 @@
     count = lax.axis_size("py")
     tables = pl.pallas_call(
         table_kernel,
-        out_shape=jax.ShapeDtypeStruct((4, 8, LANES), jnp.float32),
+        out_shape=jax.ShapeDtypeStruct((2, LANES, LANES), jnp.bfloat16),
         out_specs=vmem(1)[0],
         compiler_params=PARAMS,
         cost_estimate=pl.CostEstimate(flops=10**10, bytes_accessed=10**7, transcendentals=0),

time: 49.6 us -> 49.5 us (level)
  no operation moved by 1% of the time
where the time goes in v6:
time: 49.5 us; the launch traced here: 49.2 us
  blocking collectives  27.9 us (56%)
  starting transfers between devices  16.9 us (34%)
  Pallas kernels  2.27 us (5%)
  waiting for transfers between devices  1.45 us (3%)
  local copies, waits for them, and re-layouts  0.7 us (1%)
    ppermute x1, starting transfers between devices, shards(): halo = lax.ppermute(edge, ('px', 'py'), pairs)  16.9 us
    all_to_all x1, blocking collectives, shards(): rows = lax.all_to_all(packed, 'px', 0, 0, tiled=True).reshape(256, LANES)  16.5 us
    all_to_all x1, blocking collectives, shards(): lax.all_to_all(done.reshape(16, 8, LANES), ('lev', 'px'), 0, 0, tiled=True)  11.4 us
    ppermute x1, waiting for transfers between devices, shards(): halo = lax.ppermute(edge, ('px', 'py'), pairs)  1.45 us
    pallas_call x1, Pallas kernels, shards(): pl.pallas_call(sections_kernel, out_shape=jax.ShapeDtypeStruct((128, LANE...  1.11 us
  transfers between devices with their start and end apart: 1, of which 1 were waited for; matrix products, arithmetic and copies ran while one was open for 0% of the time, Pallas kernels for 0%

profile of v6, /device:TPU:14, one launch (start us, length us, event | category | flops | bytes accessed | tf_op | source)
XLA Modules:
  0.0 49.2 jit_solution(14605054225043066934)
XLA Ops:
  0.0 0.0 copy-start.3
  0.0 0.0 copy-start.2
  0.0 0.0 copy-start.1
  0.0 0.0 copy-start
  0.0 0.1 tables.1.first_ref.table_ref
  0.1 0.6 %copy-done.3 = f32[1,8,128]{2,1,0:T(8,128)S(1)} copy-done((f32[1,8,128]{2,1,0:T(8,128)S(1)}, f32[1,8,128]{2,1,0:T(8,128)}, u32[]{:S(2)}) %copy-start.3) | copy-done | bytes 4120
  0.7 0.0 copy-done.2
  0.7 0.0 copy-done.1
  0.7 0.1 copy-done
  0.8 0.1 pack.1
  0.9 16.5 %all_to_all.10 = f32[8,4,8,128]{3,2,1,0:T(8,128)S(1)} all-to-all(f32[8,4,8,128]{3,2,1,0:T(8,128)S(1)} %pack.1), channel_id=1, replica_groups=mesh['px'=8,'py'=64,'lev'=2] {'px'}, dimensions={0} | all-to-all | bytes 262144 | tf_op jit(solution)/shard_map/all_to_all | solution.py:274
  17.4 0.1 edge.1
  17.5 16.9 %collective-permute-start = (f32[8,8,128]{2,1,0:T(8,128)S(1)}, f32[8,8,128]{2,1,0:T(8,128)S(1)}, u32[]{:S(2)}, u32[]{:S(2)}) collective-permute-start(f32[8,8,128]{2,1,0:T(8,128)S(1)} %edge.1), channel_id=1, source_target_pairs={{4,2},{2,4},{8,6},{6,8},{12,10},{10,12},{16,14},{14,16},{20,18},{1... | collective-permute-start | bytes 98312 | tf_op jit(solution)/shard_map/ppermute | solution.py:288
  34.4 0.1 collect.1.own_ref
  34.5 1.5 %collective-permute-done.halo_ref = f32[8,8,128]{2,1,0:T(8,128)S(1)} collective-permute-done((f32[8,8,128]{2,1,0:T(8,128)S(1)}, f32[8,8,128]{2,1,0:T(8,128)S(1)}, u32[]{:S(2)}, u32[]{:S(2)}) %collective-permute-start) | collective-permute-done | bytes 32800 | tf_op jit(solution)/shard_map/ppermute | solution.py:288
  36.0 1.1 %sections.1 = f32[128,128]{1,0:T(8,128)S(1)} custom-call(f32[5,8,8,128]{3,2,1,0:T(8,128)S(1)} %collect.1.own_ref, f32[8,8,128]{2,1,0:T(8,128)S(1)} %collective-permute-done.halo_ref, bf16[2,128,128]{2,1,0:T(8,128)(2,1)S(1)} %tables.1.first_ref.table_ref), custom_call_target="tpu_custom_call" | custom-call | tf_op jit(solution)/shard_map/sections/pallas_call | solution.py:298
  37.1 0.0 copy-start.4
  37.1 11.4 %all_to_all.11.x_ref = f32[16,8,128]{2,1,0:T(8,128)S(1)} all-to-all(f32[16,8,128]{2,1,0:T(8,128)S(1)} %bitcast.4), channel_id=1, replica_groups=mesh['px'=8,'py'=64,'lev'=2] {'lev','px'}, dimensions={0} | all-to-all | bytes 131072 | tf_op jit(solution)/shard_map/all_to_all | solution.py:306
  48.5 0.0 copy-done.4
  48.5 0.7 %remap.1 = f32[2,4,8,128]{3,2,1,0:T(8,128)} custom-call(f32[2,2]{1,0:T(2,128)S(1)} %copy-done.4, f32[16,8,128]{2,1,0:T(8,128)S(1)} %all_to_all.11.x_ref), custom_call_target="tpu_custom_call" | custom-call | tf_op jit(solution)/shard_map/remap/pallas_call | solution.py:307
Async XLA Ops:
  0.0 0.7 %copy-start.3 = (f32[1,8,128]{2,1,0:T(8,128)S(1)}, f32[1,8,128]{2,1,0:T(8,128)}, u32[]{:S(2)}) copy-start(f32[1,8,128]{2,1,0:T(8,128)} %y_ref.1) | copy-start | bytes 12292
  0.0 0.7 %copy-start.2 = (f32[1,8,128]{2,1,0:T(8,128)S(1)}, f32[1,8,128]{2,1,0:T(8,128)}, u32[]{:S(2)}) copy-start(f32[1,8,128]{2,1,0:T(8,128)} %x_ref.1) | copy-start | bytes 12292
  0.0 0.7 %copy-start.1 = (f32[1,8,128]{2,1,0:T(8,128)S(1)}, f32[1,8,128]{2,1,0:T(8,128)}, u32[]{:S(2)}) copy-start(f32[1,8,128]{2,1,0:T(8,128)} %m_ref.1) | copy-start | bytes 12292
  0.0 0.8 %copy-start = (f32[1,8,8,128]{3,2,1,0:T(8,128)S(1)}, f32[1,8,8,128]{3,2,1,0:T(8,128)}, u32[]{:S(2)}) copy-start(f32[1,8,8,128]{3,2,1,0:T(8,128)} %t_ref.1) | copy-start | bytes 98308
  17.5 18.5 %collective-permute-start = (f32[8,8,128]{2,1,0:T(8,128)S(1)}, f32[8,8,128]{2,1,0:T(8,128)S(1)}, u32[]{:S(2)}, u32[]{:S(2)}) collective-permute-start(f32[8,8,128]{2,1,0:T(8,128)S(1)} %edge.1), channel_id=1, source_target_pairs={{4,2},{2,4},{8,6},{6,8},{12,10},{10,12},{16,14},{14,16},{20,18},{1... | collective-permute-start | bytes 98312 | tf_op jit(solution)/shard_map/ppermute | solution.py:288
  37.1 11.4 %copy-start.4 = (f32[2,2]{1,0:T(2,128)S(1)}, f32[2,2]{1,0:T(2,128)}, u32[]{:S(2)}) copy-start(f32[2,2]{1,0:T(2,128)} %remap_ref.1) | copy-start | bytes 52

commit v7 on v6

--- a/solution.py
+++ b/solution.py
@@ -72,17 +72,20 @@
 
 def pack_kernel(first_ref, t_ref, m_ref, x_ref, y_ref, out_ref):
     odd = lax.axis_index("py") % 2
-    window = lane_index() < WINDOW
+    lane = lane_index()
     for half in range(2):
         shift = -SLOT * half
-        piece = [rot(y_ref[0], WINDOW - SLOT * u + shift) for u in range(3)]
-        mass = jnp.where(window, rot(m_ref[0], shift), piece[2])
-        wind = rot(x_ref[0], shift)
+        turn = [HALO * u + (HALO - WINDOW) * half for u in range(4)]
+        window = [(lane + LANES - turn[u]) % LANES < WINDOW for u in range(4)]
+        piece = [rot(y_ref[0], WINDOW - SLOT * u + shift + turn[u]) for u in range(3)]
+        mass = jnp.where(window[2], rot(m_ref[0], shift + turn[2]), piece[2])
+        last = rot(y_ref[0], HALO + shift + turn[3])
+        wind = jnp.where(window[3], rot(x_ref[0], shift + turn[3]), last)
         place = jnp.where(odd == 1, 1 - half, half)
         for q in range(4):
             for u in range(2):
-                t = rot(t_ref[0, 2 * q + u], shift)
-                out_ref[2 * q + place, u] = jnp.where(window, t, piece[u])
+                t = rot(t_ref[0, 2 * q + u], shift + turn[u])
+                out_ref[2 * q + place, u] = jnp.where(window[u], t, piece[u])
             out_ref[2 * q + place, 2] = mass
             out_ref[2 * q + place, 3] = wind
 
@@ -104,17 +107,20 @@
     left = works_left()
     for r in range(8):
         unit = [gathered(r_ref, u, r) for u in range(4)]
-        edge = moved_lanes(jnp.where(left, unit[0], unit[2]), left, 0, -8)
+        edge = jnp.where(left, unit[0], unit[3])
         for a in range(4):
-            piece = moved_lanes(unit[a], left, HALO * a, HALO * a + HALO - WINDOW)
-            edge = jnp.where(slot == a, piece, edge)
+            edge = jnp.where(slot == a, unit[a], edge)
         out_ref[r] = edge
 
 
 def collect_kernel(r_ref, out_ref):
     lane = lane_index()
+    left = works_left()
     for r in range(8):
-        unit = [gathered(r_ref, u, r) for u in range(4)]
+        unit = [
+            moved_lanes(gathered(r_ref, u, r), left, -HALO * u, WINDOW - HALO - HALO * u)
+            for u in range(4)
+        ]
         last = jnp.where(lane < 2 * SLOT, rot(unit[1], 2 * SLOT), rot(unit[2], 3 * SLOT))
         last = jnp.where(lane < SLOT, rot(unit[0], SLOT), last)
         for a in range(4):

time: 49.5 us -> 49.4 us (level)
  no operation moved by 1% of the time
where the time goes in v7:
time: 49.4 us; the launch traced here: 49.2 us
  blocking collectives  27.9 us (56%)
  starting transfers between devices  16.9 us (34%)
  Pallas kernels  2.28 us (5%)
  waiting for transfers between devices  1.38 us (3%)
  local copies, waits for them, and re-layouts  0.7 us (1%)
    ppermute x1, starting transfers between devices, shards(): halo = lax.ppermute(edge, ('px', 'py'), pairs)  16.9 us
    all_to_all x1, blocking collectives, shards(): rows = lax.all_to_all(packed, 'px', 0, 0, tiled=True).reshape(256, LANES)  16.5 us
    all_to_all x1, blocking collectives, shards(): lax.all_to_all(done.reshape(16, 8, LANES), ('lev', 'px'), 0, 0, tiled=True)  11.4 us
    ppermute x1, waiting for transfers between devices, shards(): halo = lax.ppermute(edge, ('px', 'py'), pairs)  1.38 us
    pallas_call x1, Pallas kernels, shards(): pl.pallas_call(sections_kernel, out_shape=jax.ShapeDtypeStruct((128, LANE...  1.11 us
  transfers between devices with their start and end apart: 1, of which 1 were waited for; matrix products, arithmetic and copies ran while one was open for 0% of the time, Pallas kernels for 0%

profile of v7, /device:TPU:14, one launch (start us, length us, event | category | flops | bytes accessed | tf_op | source)
XLA Modules:
  0.0 49.2 jit_solution(5278012811472720064)
XLA Ops:
  0.0 0.0 copy-start.3
  0.0 0.0 copy-start.2
  0.0 0.0 copy-start.1
  0.0 0.0 copy-start
  0.0 0.1 tables.1.first_ref.table_ref
  0.1 0.6 %copy-done.3 = f32[1,8,128]{2,1,0:T(8,128)S(1)} copy-done((f32[1,8,128]{2,1,0:T(8,128)S(1)}, f32[1,8,128]{2,1,0:T(8,128)}, u32[]{:S(2)}) %copy-start.3) | copy-done | bytes 4120
  0.7 0.0 copy-done.2
  0.7 0.0 copy-done.1
  0.7 0.1 copy-done
  0.8 0.1 pack.1
  0.9 16.5 %all_to_all.10 = f32[8,4,8,128]{3,2,1,0:T(8,128)S(1)} all-to-all(f32[8,4,8,128]{3,2,1,0:T(8,128)S(1)} %pack.1), channel_id=1, replica_groups=mesh['px'=8,'py'=64,'lev'=2] {'px'}, dimensions={0} | all-to-all | bytes 262144 | tf_op jit(solution)/shard_map/all_to_all | solution.py:280
  17.4 0.1 edge.1
  17.4 16.9 %collective-permute-start = (f32[8,8,128]{2,1,0:T(8,128)S(1)}, f32[8,8,128]{2,1,0:T(8,128)S(1)}, u32[]{:S(2)}, u32[]{:S(2)}) collective-permute-start(f32[8,8,128]{2,1,0:T(8,128)S(1)} %edge.1), channel_id=1, source_target_pairs={{4,2},{2,4},{8,6},{6,8},{12,10},{10,12},{16,14},{14,16},{20,18},{1... | collective-permute-start | bytes 98312 | tf_op jit(solution)/shard_map/ppermute | solution.py:294
  34.3 0.2 collect.1.own_ref
  34.5 1.4 %collective-permute-done.halo_ref = f32[8,8,128]{2,1,0:T(8,128)S(1)} collective-permute-done((f32[8,8,128]{2,1,0:T(8,128)S(1)}, f32[8,8,128]{2,1,0:T(8,128)S(1)}, u32[]{:S(2)}, u32[]{:S(2)}) %collective-permute-start) | collective-permute-done | bytes 32800 | tf_op jit(solution)/shard_map/ppermute | solution.py:294
  35.9 1.1 %sections.1 = f32[128,128]{1,0:T(8,128)S(1)} custom-call(f32[5,8,8,128]{3,2,1,0:T(8,128)S(1)} %collect.1.own_ref, f32[8,8,128]{2,1,0:T(8,128)S(1)} %collective-permute-done.halo_ref, bf16[2,128,128]{2,1,0:T(8,128)(2,1)S(1)} %tables.1.first_ref.table_ref), custom_call_target="tpu_custom_call" | custom-call | tf_op jit(solution)/shard_map/sections/pallas_call | solution.py:304
  37.0 0.0 copy-start.4
  37.0 11.4 %all_to_all.11.x_ref = f32[16,8,128]{2,1,0:T(8,128)S(1)} all-to-all(f32[16,8,128]{2,1,0:T(8,128)S(1)} %bitcast.4), channel_id=1, replica_groups=mesh['px'=8,'py'=64,'lev'=2] {'lev','px'}, dimensions={0} | all-to-all | bytes 131072 | tf_op jit(solution)/shard_map/all_to_all | solution.py:312
  48.4 0.0 copy-done.4
  48.4 0.7 %remap.1 = f32[2,4,8,128]{3,2,1,0:T(8,128)} custom-call(f32[2,2]{1,0:T(2,128)S(1)} %copy-done.4, f32[16,8,128]{2,1,0:T(8,128)S(1)} %all_to_all.11.x_ref), custom_call_target="tpu_custom_call" | custom-call | tf_op jit(solution)/shard_map/remap/pallas_call | solution.py:313
Async XLA Ops:
  0.0 0.7 %copy-start.3 = (f32[1,8,128]{2,1,0:T(8,128)S(1)}, f32[1,8,128]{2,1,0:T(8,128)}, u32[]{:S(2)}) copy-start(f32[1,8,128]{2,1,0:T(8,128)} %y_ref.1) | copy-start | bytes 12292
  0.0 0.7 %copy-start.2 = (f32[1,8,128]{2,1,0:T(8,128)S(1)}, f32[1,8,128]{2,1,0:T(8,128)}, u32[]{:S(2)}) copy-start(f32[1,8,128]{2,1,0:T(8,128)} %x_ref.1) | copy-start | bytes 12292
  0.0 0.7 %copy-start.1 = (f32[1,8,128]{2,1,0:T(8,128)S(1)}, f32[1,8,128]{2,1,0:T(8,128)}, u32[]{:S(2)}) copy-start(f32[1,8,128]{2,1,0:T(8,128)} %m_ref.1) | copy-start | bytes 12292
  0.0 0.8 %copy-start = (f32[1,8,8,128]{3,2,1,0:T(8,128)S(1)}, f32[1,8,8,128]{3,2,1,0:T(8,128)}, u32[]{:S(2)}) copy-start(f32[1,8,8,128]{3,2,1,0:T(8,128)} %t_ref.1) | copy-start | bytes 98308
  17.4 18.5 %collective-permute-start = (f32[8,8,128]{2,1,0:T(8,128)S(1)}, f32[8,8,128]{2,1,0:T(8,128)S(1)}, u32[]{:S(2)}, u32[]{:S(2)}) collective-permute-start(f32[8,8,128]{2,1,0:T(8,128)S(1)} %edge.1), channel_id=1, source_target_pairs={{4,2},{2,4},{8,6},{6,8},{12,10},{10,12},{16,14},{14,16},{20,18},{1... | collective-permute-start | bytes 98312 | tf_op jit(solution)/shard_map/ppermute | solution.py:294
  37.0 11.4 %copy-start.4 = (f32[2,2]{1,0:T(2,128)S(1)}, f32[2,2]{1,0:T(2,128)}, u32[]{:S(2)}) copy-start(f32[2,2]{1,0:T(2,128)} %remap_ref.1) | copy-start | bytes 52
